TPU v7x, 128 devices: a whole 4x4x4 slice. The times are simulated.
128 devices in a mesh: row: 16 (over z, y), col: 8 (over x, core).
Axes of the slice: x: 4, y: 4, z: 4, core: 2. Of those that a mesh axis runs over, the one named last changes fastest.
Arguments:
- tiles: bfloat16 [1024, 64, 128, 128], P('row', 'col'), may hold values from -0.0625 to 0.0625
- tile_cols: int32 [1024, 64], P('row', 'col'), may hold values from 0 to 63
- counts: int32 [1024, 8], P('row', 'col'), may hold values from 1 to 8
- scales: float32 [1024, 64], P('row', 'col'), may hold values from 0.5 to 6
- sketch: bfloat16 [65536, 256], P('col'), may hold values from -6 to 6
Outputs:
- basis: float32 [131072, 256], P(('row', 'col'))
- r_factor: float32 [256, 256], replicated
All inputs are finite; a program needn't handle non-finite values.
Results may differ from a plain program's by a relative error of at most 0.0029.
Values sent between devices are 32-bit elements; how exact they have to be, the bound alone decides.
No kernel may reach another device: no remote copies, remote signals or barrier semaphores. Data moves between devices by JAX's collectives and lax.ppermute only.
A program may use at most 192 MiB of HBM per device.

v0:
```python
import functools

import jax
import jax.numpy as jnp
from jax import lax
from jax.experimental import pallas as pl
from jax.experimental.pallas import tpu as pltpu
from jax.sharding import PartitionSpec as P


F32 = jnp.float32
BF16 = jnp.bfloat16
RB = 4
SLOTS = 8
T = 128
K = 256
HALF = RB * T
VMEM_LIMIT = 16 << 20
SKETCH_PIECES = 16


def split(a):
    hi = a.astype(BF16)
    return hi, (a - hi.astype(F32)).astype(BF16)


def dot(a, b, dims=((1,), (0,))):
    return lax.dot_general(a, b, (dims, ((), ())), preferred_element_type=F32)


def dot3(a, b, dims=((1,), (0,))):
    ah, al = split(a)
    bh, bl = split(b)
    return dot(ah, bh, dims) + (dot(ah, bl, dims) + dot(al, bh, dims))


def first_row(item):
    dx, flip, half = item
    me = lax.axis_index("col")
    return ((((me >> 1) + dx) & 3) * 2 + ((me + flip) & 1)) * 2 * RB + half * RB


def block_row(row, tile, cols, counts, scales, sketch):
    live = counts[0, row]
    dense = []
    blocks = []
    for s in range(SLOTS):
        scale = jnp.where(s < live, scales[s, row], 0.0)
        dense.append((tile(s).astype(F32) * scale).astype(BF16))
        start = pl.multiple_of(cols[s, row] * T, T)
        blocks.append(sketch[pl.ds(start, T), :])
    return dot(jnp.concatenate(dense, axis=1), jnp.concatenate(blocks, axis=0))


def first_kernel(items, kept, cols, counts, scales, tiles, sketch, *refs):
    n = len(items)
    outs, (held, local), (tile_sem, held_sem, sketch_sem) = refs[:n], refs[n:n + 2], refs[n + 3:]
    buf = refs[n + 2]
    piece = local.shape[0] // SKETCH_PIECES
    load = []
    for j in range(SKETCH_PIECES):
        rows = pl.ds(j * piece, piece)
        load.append(pltpu.make_async_copy(sketch.at[rows], local.at[rows], sketch_sem.at[j]))
    tile_load, held_load = [], []
    for group, into, sem, out in ((items, buf, tile_sem, tile_load), (kept, held, held_sem, held_load)):
        for i, item in enumerate(group):
            for r in range(RB):
                for p in range(2):
                    part = pl.ds(p * (SLOTS // 2), SLOTS // 2)
                    to = i * RB + r
                    out.append(pltpu.make_async_copy(
                        tiles.at[first_row(item) + r, part], into.at[to, part], sem.at[2 * to + p]
                    ))
    for copy in load + tile_load + held_load:
        copy.start()
    for copy in load:
        copy.wait()
    for i, item in enumerate(items):
        for r in range(RB):
            to = i * RB + r
            tile_load[2 * to].wait()
            tile_load[2 * to + 1].wait()
            outs[i][r * T:(r + 1) * T, :] = block_row(
                first_row(item) + r, lambda s: buf[to, s], cols, counts, scales, local
            )
    for copy in held_load:
        copy.wait()


def first(items, kept, meta, tiles, sketch):
    vmem = pl.BlockSpec(memory_space=pltpu.VMEM)
    smem = pl.BlockSpec(memory_space=pltpu.SMEM)
    hbm = pl.BlockSpec(memory_space=pltpu.HBM)
    rows, keep = RB * len(items), RB * len(kept)
    return pl.pallas_call(
        functools.partial(first_kernel, items, kept),
        in_specs=[smem] * 3 + [hbm] * 2,
        out_specs=[vmem] * (len(items) + 2),
        out_shape=[jax.ShapeDtypeStruct((HALF, K), F32)] * len(items)
        + [
            jax.ShapeDtypeStruct((keep, SLOTS, T, T), BF16),
            jax.ShapeDtypeStruct(sketch.shape, BF16),
        ],
        scratch_shapes=[
            pltpu.VMEM((rows, SLOTS, T, T), BF16),
            pltpu.SemaphoreType.DMA((2 * rows,)),
            pltpu.SemaphoreType.DMA((2 * keep,)),
            pltpu.SemaphoreType.DMA((SKETCH_PIECES,)),
        ],
        compiler_params=pltpu.CompilerParams(vmem_limit_bytes=VMEM_LIMIT),
        cost_estimate=pl.CostEstimate(
            flops=2 * len(items) * HALF * SLOTS * T * K, bytes_accessed=8 << 20, transcendentals=0
        ),
        name="first",
    )(*meta, tiles, sketch)


def spmm_kernel(items, joins, waits, held, cols, counts, scales, tiles, sketch, *refs):
    adds = refs[:joins]
    outs = refs[joins + waits:]
    for n, item in enumerate(items):
        base = first_row(item)
        for r in range(RB):
            at = held * RB + n * RB + r if held is not None else base + r
            acc = block_row(base + r, lambda s: tiles[at, s], cols, counts, scales, sketch)
            rows = slice(r * T, (r + 1) * T)
            for j in range(n, joins, len(items)):
                acc = acc + adds[j][rows, :]
            outs[n][rows, :] = acc


def spmm(items, meta, tiles, sketch, adds=(), after=(), held=None):
    vmem = pl.BlockSpec(memory_space=pltpu.VMEM)
    smem = pl.BlockSpec(memory_space=pltpu.SMEM)
    anywhere = pl.BlockSpec(memory_space=pl.ANY)
    return pl.pallas_call(
        functools.partial(spmm_kernel, items, len(adds), len(after), held),
        in_specs=[smem] * 3 + [vmem] * (2 + len(adds)) + [anywhere] * len(after),
        out_specs=[vmem] * len(items),
        out_shape=[jax.ShapeDtypeStruct((HALF, K), F32)] * len(items),
        compiler_params=pltpu.CompilerParams(vmem_limit_bytes=VMEM_LIMIT),
        cost_estimate=pl.CostEstimate(
            flops=2 * len(items) * HALF * SLOTS * T * K, bytes_accessed=4 << 20, transcendentals=0
        ),
        name="spmm",
    )(*meta, tiles, sketch, *adds, *after)


PACK = 272
PH = PACK // 2


def gram_kernel(s0, s1, vp, um, up, vm, prod, keep, send, acc, pack):
    chunk = 256
    core = lax.axis_index("col") & 1
    for j in range(1024 // chunk):
        h, o = divmod(j * chunk, HALF)
        rows = slice(o, o + chunk)
        first, second = ((vp, um), (up, vm))[h]
        p = (s0, s1)[h][rows, :] + (first[rows, :] + second[rows, :])
        prod[j * chunk:(j + 1) * chunk, :] = p
        hi, lo = split(p)
        main = dot(hi, hi, ((0,), (0,)))
        cross = dot(hi, lo, ((0,), (0,)))
        if j == 0:
            acc[0] = main
            acc[1] = cross
        else:
            acc[0] += main
            acc[1] += cross
    g = acc[0] + (acc[1] + acc[1].T)
    low = g[T:, T:]
    r = lax.broadcasted_iota(jnp.int32, (T, T), 0)
    c = lax.broadcasted_iota(jnp.int32, (T, T), 1)
    pack[0:T, :] = jnp.where(r >= c, g[:T, :T], low)
    pack[T:K, :] = g[T:, :T]
    diag = jnp.sum(jnp.where(r == c, low, 0.0), axis=0, keepdims=True)
    pack[K:PACK, :] = jnp.broadcast_to(diag, (PACK - K, T))

    @pl.when(core == 0)
    def _():
        keep[...] = pack[:PH, :]
        send[...] = pack[PH:, :]

    @pl.when(core == 1)
    def _():
        keep[...] = pack[PH:, :]
        send[...] = pack[:PH, :]


def gram(s0, s1, vp, um, up, vm):
    vmem = pl.BlockSpec(memory_space=pltpu.VMEM)
    return pl.pallas_call(
        gram_kernel,
        in_specs=[vmem] * 6,
        out_specs=[vmem] * 3,
        scratch_shapes=[pltpu.VMEM((2, K, K), F32), pltpu.VMEM((PACK, T), F32)],
        out_shape=[jax.ShapeDtypeStruct((2 * HALF, K), F32)]
        + [jax.ShapeDtypeStruct((PH, T), F32)] * 2,
        compiler_params=pltpu.CompilerParams(vmem_limit_bytes=VMEM_LIMIT),
        name="gram",
    )(s0, s1, vp, um, up, vm)


def basis_kernel(root, mine, other, prod, basis, rfac, pack, a_ref, w_ref, e_ref):
    core = lax.axis_index("col") & 1

    @pl.when(core == 0)
    def _():
        pack[:PH, :] = mine[...]
        pack[PH:, :] = other[...]

    @pl.when(core == 1)
    def _():
        pack[:PH, :] = other[...]
        pack[PH:, :] = mine[...]

    r = lax.broadcasted_iota(jnp.int32, (T, T), 0)
    c = lax.broadcasted_iota(jnp.int32, (T, T), 1)
    m = pack[0:T, :]
    mt = m.T
    b = pack[T:K, :]
    a_ref[:T, :T] = jnp.where(r >= c, m, mt)
    a_ref[T:, :T] = b
    a_ref[:T, T:] = b.T
    a_ref[T:, T:] = jnp.where(r < c, m, jnp.where(r > c, mt, pack[K:K + 1, :]))

    rr = lax.broadcasted_iota(jnp.int32, (K, K), 0)
    cc = lax.broadcasted_iota(jnp.int32, (K, K), 1)
    eye = rr == cc
    a = a_ref[...]
    masked = jnp.where(eye, a, 0.0)
    dcol = lax.rsqrt(jnp.sum(masked, axis=1, keepdims=True))
    drow = lax.rsqrt(jnp.sum(masked, axis=0, keepdims=True))
    unit = jnp.where(eye, 0.0, a * dcol * drow)
    e_ref[...] = unit
    w_ref[...] = jnp.where(eye, 1.0, 0.0)

    def size(e):
        return jnp.max(jnp.sum(jnp.abs(e), axis=0, keepdims=True))

    def update(e):
        phi = jnp.where(rr > cc, e, jnp.where(eye, 0.5 * e, 0.0)).astype(BF16)
        w = w_ref[...]
        t = dot(phi, w.astype(BF16))
        w_ref[...] = w - t + dot(phi, t.astype(BF16))

    def cond(state):
        it, err = state
        return jnp.logical_and(err >= 0.01, it < 10)

    def body(state):
        it, _ = state
        update(e_ref[...])
        w = w_ref[...]
        scaled = jnp.where(eye, 1.0, unit)
        t = dot3(w, scaled)
        e = dot3(t, w, ((1,), (1,))) - jnp.where(eye, 1.0, 0.0)
        e_ref[...] = e
        return it + 1, size(e)

    _, err = lax.while_loop(cond, body, (jnp.int32(0), size(unit)))
    good = err < 0.01

    @pl.when(good)
    def _():
        update(e_ref[...])
        w_ref[...] = w_ref[...] * drow

    @pl.when(jnp.logical_not(good))
    def _():
        w_ref[...] = jnp.where(eye, 1.0, 0.0)
        e_ref[...] = a_ref[...]
        lane = lax.broadcasted_iota(jnp.int32, (1, K), 1)

        def step(k, carry):
            arow = e_ref[pl.ds(k, 1), :]
            wrow = w_ref[pl.ds(k, 1), :]
            inv = lax.rsqrt(jnp.sum(jnp.where(lane == k, arow, 0.0), axis=1, keepdims=True))
            arow = arow * inv
            wrow = wrow * inv
            full = e_ref[...]
            col = jnp.sum(jnp.where(cc == k, full, 0.0), axis=1, keepdims=True) * inv
            col = jnp.where(rr[:, :1] > k, col, 0.0)
            e_ref[...] = full - col * arow
            w_ref[...] = w_ref[...] - col * wrow
            w_ref[pl.ds(k, 1), :] = wrow
            return carry

        lax.fori_loop(0, K, step, 0)

    w = w_ref[...]
    upper = dot3(w, a_ref[...])
    rfac[...] = jnp.where(rr <= cc, upper, 0.0) * (1.0 / root)
    wh, wl = split(w * root)
    for j in range(4):
        rows = slice(j * 256, (j + 1) * 256)
        ph, plo = split(prod[rows, :])
        dims = ((1,), (1,))
        basis[rows, :] = dot(ph, wh, dims) + (dot(ph, wl, dims) + dot(plo, wh, dims))


def finish(root, mine, other, prod):
    vmem = pl.BlockSpec(memory_space=pltpu.VMEM)
    return pl.pallas_call(
        functools.partial(basis_kernel, root),
        in_specs=[vmem] * 3,
        out_specs=[vmem] * 2,
        scratch_shapes=[pltpu.VMEM((PACK, T), F32)] + [pltpu.VMEM((K, K), F32)] * 3,
        out_shape=[
            jax.ShapeDtypeStruct((2 * HALF, K), F32),
            jax.ShapeDtypeStruct((K, K), F32),
        ],
        compiler_params=pltpu.CompilerParams(vmem_limit_bytes=VMEM_LIMIT),
        name="finish",
    )(mine, other, prod)


def perm(size, target):
    return [(i, target(i)) for i in range(size)]


def on_device(tiles, tile_cols, counts, scales, sketch):
    rows_all = tiles.shape[0] * T * lax.axis_size("row")
    meta = tuple(
        pltpu.with_memory_space_constraint(a, pltpu.HBM) for a in (tile_cols.T, counts.T, scales.T)
    )
    partner = perm(8, lambda c: c ^ 1)
    plus = perm(8, lambda c: (c + 2) % 8)
    minus = perm(8, lambda c: (c + 6) % 8)

    def move(q, to):
        return lax.ppermute(q, "col", to)

    qa, qb, held, local = first(
        ((2, 1, 0), (2, 1, 1)),
        ((2, 0, 0), (2, 0, 1)),
        meta,
        pltpu.with_memory_space_constraint(tiles, pltpu.HBM),
        pltpu.with_memory_space_constraint(sketch, pltpu.HBM),
    )
    later, _ = lax.optimization_barrier((tiles, qa))
    near = pltpu.with_memory_space_constraint(later, pltpu.VMEM)

    def sp(*items, tiles=near, **kw):
        return spmm(items, meta, tiles, local, **kw)

    ca, cb = move(qa, partner), move(qb, partner)
    (d2p,) = sp((2, 0, 0), tiles=held, held=0, adds=(ca,))
    tp = move(d2p, plus)
    (d2m,) = sp((2, 0, 1), tiles=held, held=1, adds=(cb,), after=(d2p,))
    tm = move(d2m, minus)
    qu = sp((1, 1, 1), (3, 1, 0), after=(d2m,))
    cu = [move(q, partner) for q in qu]
    qv = sp((1, 1, 0), (3, 1, 1), after=qu)
    cv = [move(q, partner) for q in qv]
    up, um = sp((1, 0, 1), (3, 0, 0), adds=cu, after=qv)
    mid = up
    up, um = move(up, plus), move(um, minus)
    qo = sp((0, 1, 0), (0, 1, 1), after=(mid,))
    co = [move(q, partner) for q in qo]
    vp, vm = sp((1, 0, 0), (3, 0, 1), adds=(*cv, tp, tm), after=qo)
    last = vp
    vp, vm = move(vp, plus), move(vm, minus)
    s0, s1 = sp((0, 0, 0), (0, 0, 1), adds=co, after=(last,))

    prod, keep, send = gram(s0, s1, vp, um, up, vm)
    tot = keep + move(send, partner)
    even = lambda v: v ^ 1
    odd = lambda v: (v + (1 if v % 2 else 3)) % 4
    for pair in (even, odd):
        tot = tot + lax.ppermute(tot, "col", perm(8, lambda c: pair(c // 2) * 2 + c % 2))
        tot = tot + lax.ppermute(tot, "row", perm(16, lambda r: r // 4 * 4 + pair(r % 4)))
        tot = tot + lax.ppermute(tot, "row", perm(16, lambda r: pair(r // 4) * 4 + r % 4))
    rest = move(tot, partner)
    basis, rfac = finish(float(rows_all) ** 0.5, tot, rest, prod)
    return basis, rfac


def solution(mesh):
    in_specs = (
        P("row", "col", None, None),
        P("row", "col"),
        P("row", "col"),
        P("row", "col"),
        P("col", None),
    )
    out_specs = (P(("row", "col"), None), P())

    return jax.shard_map(
        on_device, mesh=mesh, in_specs=in_specs, out_specs=out_specs, check_vma=False
    )
```

profile of v0, /device:TPU:1, one launch (start us, length us, event | category | flops | bytes accessed | tf_op | source)
XLA Modules:
  0.0 135.4 jit_solution(7589467948465563896)
XLA Ops:
  0.7 7.4 %first.1 = (f32[512,256]{1,0:T(8,128)S(1)}, f32[512,256]{1,0:T(8,128)S(1)}, bf16[8,8,128,128]{3,2,1,0:T(8,128)(2,1)S(1)}, bf16[8192,256]{1,0:T(8,128)(2,1)S(1)}) custom-call(s32[8,64]{1,0:T(8,128)} %bitcast.5, s32[1,64]{1,0:T(1,128)} %bitcast.23, f32[8,64]{1,0:T(8,128)} %bitcast.14, bf16[64,8,128,128]{3,2,1,0:T(8,128)(2,1)} %tiles.7, bf16[8192,256]{1,0:T(8,128)(2,1)} %sketch.1), custom_call_target="tpu_custom_call" | custom-call | flops 536870912 | bytes 8388608 | tf_op jit(solution)/shard_map/first/pallas_call | solution.py:95
  15.9 2.6 %collective-permute-start.9 = (f32[512,256]{1,0:T(8,128)S(1)}, f32[512,256]{1,0:T(8,128)S(1)}, u32[]{:S(2)}, u32[]{:S(2)}) collective-permute-start(f32[512,256]{1,0:T(8,128)S(1)} %spmm.9.refs_0_), channel_id=1, source_target_pairs={{0,6},{1,7},{2,0},{3,1},{4,2},{5,3},{6,4},{7,5},{8,14},{9,15},{10,... | collective-permute-start | bytes 1572872 | tf_op jit(solution)/shard_map/ppermute | solution.py:333
  22.4 1.5 %spmm.13 = (f32[512,256]{1,0:T(8,128)S(1)}, f32[512,256]{1,0:T(8,128)S(1)}) custom-call(s32[8,64]{1,0:T(8,128)} %bitcast.11, s32[1,64]{1,0:T(1,128)} %bitcast.29, f32[8,64]{1,0:T(8,128)} %bitcast.20, bf16[64,8,128,128]{3,2,1,0:T(8,128)(2,1)S(1)} %bitcast.4, bf16[8192,256]{1,0:T(8,128)(2,1)S(1)} %get-tuple-element.24.sketch, ...), custom_call_target="tpu_custom_call" | custom-call | flops 536870912 | bytes 4194304 | tf_op jit(solution)/shard_map/spmm/pallas_call | solution.py:136
  24.5 5.0 %collective-permute-done.9.refs_3_ = f32[512,256]{1,0:T(8,128)S(1)} collective-permute-done((f32[512,256]{1,0:T(8,128)S(1)}, f32[512,256]{1,0:T(8,128)S(1)}, u32[]{:S(2)}, u32[]{:S(2)}) %collective-permute-start.9) | collective-permute-done | bytes 524320 | tf_op jit(solution)/shard_map/ppermute | solution.py:333
  30.4 2.2 %collective-permute-done.8.refs_2_ = f32[512,256]{1,0:T(8,128)S(1)} collective-permute-done((f32[512,256]{1,0:T(8,128)S(1)}, f32[512,256]{1,0:T(8,128)S(1)}, u32[]{:S(2)}, u32[]{:S(2)}) %collective-permute-start.8) | collective-permute-done | bytes 524320 | tf_op jit(solution)/shard_map/ppermute | solution.py:333
  34.4 1.5 %spmm.14 = (f32[512,256]{1,0:T(8,128)S(1)}, f32[512,256]{1,0:T(8,128)S(1)}) custom-call(s32[8,64]{1,0:T(8,128)} %bitcast.12, s32[1,64]{1,0:T(1,128)} %bitcast.30, f32[8,64]{1,0:T(8,128)} %bitcast.21, bf16[64,8,128,128]{3,2,1,0:T(8,128)(2,1)S(1)} %bitcast.4, bf16[8192,256]{1,0:T(8,128)(2,1)S(1)} %get-tuple-element.24.sketch, ...), custom_call_target="tpu_custom_call" | custom-call | flops 536870912 | bytes 4194304 | tf_op jit(solution)/shard_map/spmm/pallas_call | solution.py:136
  35.9 1.8 %collective-permute-start.13 = (f32[512,256]{1,0:T(8,128)S(1)}, f32[512,256]{1,0:T(8,128)S(1)}, u32[]{:S(2)}, u32[]{:S(2)}) collective-permute-start(f32[512,256]{1,0:T(8,128)S(1)} %get-tuple-element.38), channel_id=1, source_target_pairs={{0,6},{1,7},{2,0},{3,1},{4,2},{5,3},{6,4},{7,5},{8,14},{9,15},{10,... | collective-permute-start | bytes 1572872 | tf_op jit(solution)/shard_map/ppermute | solution.py:333
  37.7 1.5 %spmm.15 = (f32[512,256]{1,0:T(8,128)S(1)}, f32[512,256]{1,0:T(8,128)S(1)}) custom-call(s32[8,64]{1,0:T(8,128)} %bitcast.13, s32[1,64]{1,0:T(1,128)} %bitcast.31, f32[8,64]{1,0:T(8,128)} %bitcast.22, bf16[64,8,128,128]{3,2,1,0:T(8,128)(2,1)S(1)} %bitcast.4, bf16[8192,256]{1,0:T(8,128)(2,1)S(1)} %get-tuple-element.24.sketch, ...), custom_call_target="tpu_custom_call" | custom-call | flops 536870912 | bytes 4194304 | tf_op jit(solution)/shard_map/spmm/pallas_call | solution.py:136
  39.3 5.3 %collective-permute-done.11.um = f32[512,256]{1,0:T(8,128)S(1)} collective-permute-done((f32[512,256]{1,0:T(8,128)S(1)}, f32[512,256]{1,0:T(8,128)S(1)}, u32[]{:S(2)}, u32[]{:S(2)}) %collective-permute-start.11) | collective-permute-done | bytes 524320 | tf_op jit(solution)/shard_map/ppermute | solution.py:333
  44.6 11.2 %collective-permute-done.13.vm = f32[512,256]{1,0:T(8,128)S(1)} collective-permute-done((f32[512,256]{1,0:T(8,128)S(1)}, f32[512,256]{1,0:T(8,128)S(1)}, u32[]{:S(2)}, u32[]{:S(2)}) %collective-permute-start.13) | collective-permute-done | bytes 524320 | tf_op jit(solution)/shard_map/ppermute | solution.py:333
  56.4 2.4 %collective-permute-start.14 = (f32[136,128]{1,0:T(8,128)S(1)}, f32[136,128]{1,0:T(8,128)S(1)}, u32[]{:S(2)}, u32[]{:S(2)}) collective-permute-start(f32[136,128]{1,0:T(8,128)S(1)} %get-tuple-element.40), channel_id=1, source_target_pairs={{0,1},{1,0},{2,3},{3,2},{4,5},{5,4},{6,7},{7,6},{8,9},{9,8},{10,11... | collective-permute-start | bytes 208904 | tf_op jit(solution)/shard_map/ppermute | solution.py:333
  59.9 3.1 %collective-permute-done.15 = f32[136,128]{1,0:T(8,128)S(1)} collective-permute-done((f32[136,128]{1,0:T(8,128)S(1)}, f32[136,128]{1,0:T(8,128)S(1)}, u32[]{:S(2)}, u32[]{:S(2)}) %collective-permute-start.15) | collective-permute-done | bytes 69664 | tf_op jit(solution)/shard_map/ppermute | solution.py:372
  63.0 1.6 %collective-permute-start.16 = (f32[136,128]{1,0:T(8,128)S(1)}, f32[136,128]{1,0:T(8,128)S(1)}, u32[]{:S(2)}, u32[]{:S(2)}) collective-permute-start(f32[136,128]{1,0:T(8,128)S(1)} %add.22), channel_id=1, source_target_pairs={{0,8},{8,0},{16,24},{24,16},{32,40},{40,32},{48,56},{56,48},{64,72... | collective-permute-start | bytes 208904 | tf_op jit(solution)/shard_map/ppermute | solution.py:373
  64.6 1.9 %collective-permute-done.16 = f32[136,128]{1,0:T(8,128)S(1)} collective-permute-done((f32[136,128]{1,0:T(8,128)S(1)}, f32[136,128]{1,0:T(8,128)S(1)}, u32[]{:S(2)}, u32[]{:S(2)}) %collective-permute-start.16) | collective-permute-done | bytes 69664 | tf_op jit(solution)/shard_map/ppermute | solution.py:373
  66.5 1.7 %collective-permute-start.17 = (f32[136,128]{1,0:T(8,128)S(1)}, f32[136,128]{1,0:T(8,128)S(1)}, u32[]{:S(2)}, u32[]{:S(2)}) collective-permute-start(f32[136,128]{1,0:T(8,128)S(1)} %add.23), channel_id=1, source_target_pairs={{0,32},{8,40},{16,48},{24,56},{32,0},{40,8},{48,16},{56,24},{64,96... | collective-permute-start | bytes 208904 | tf_op jit(solution)/shard_map/ppermute | solution.py:374
  68.2 1.7 %collective-permute-done.17 = f32[136,128]{1,0:T(8,128)S(1)} collective-permute-done((f32[136,128]{1,0:T(8,128)S(1)}, f32[136,128]{1,0:T(8,128)S(1)}, u32[]{:S(2)}, u32[]{:S(2)}) %collective-permute-start.17) | collective-permute-done | bytes 69664 | tf_op jit(solution)/shard_map/ppermute | solution.py:374
  69.9 1.6 %collective-permute-start.18 = (f32[136,128]{1,0:T(8,128)S(1)}, f32[136,128]{1,0:T(8,128)S(1)}, u32[]{:S(2)}, u32[]{:S(2)}) collective-permute-start(f32[136,128]{1,0:T(8,128)S(1)} %add.24), channel_id=1, source_target_pairs={{0,6},{1,7},{2,4},{3,5},{4,2},{5,3},{6,0},{7,1},{8,14},{9,15},{10,... | collective-permute-start | bytes 208904 | tf_op jit(solution)/shard_map/ppermute | solution.py:372
  71.5 2.9 %collective-permute-done.18 = f32[136,128]{1,0:T(8,128)S(1)} collective-permute-done((f32[136,128]{1,0:T(8,128)S(1)}, f32[136,128]{1,0:T(8,128)S(1)}, u32[]{:S(2)}, u32[]{:S(2)}) %collective-permute-start.18) | collective-permute-done | bytes 69664 | tf_op jit(solution)/shard_map/ppermute | solution.py:372
  74.4 2.8 %collective-permute-start.19 = (f32[136,128]{1,0:T(8,128)S(1)}, f32[136,128]{1,0:T(8,128)S(1)}, u32[]{:S(2)}, u32[]{:S(2)}) collective-permute-start(f32[136,128]{1,0:T(8,128)S(1)} %add.25), channel_id=1, source_target_pairs={{0,24},{8,16},{16,8},{24,0},{32,56},{40,48},{48,40},{56,32},{64,88... | collective-permute-start | bytes 208904 | tf_op jit(solution)/shard_map/ppermute | solution.py:373
  77.2 1.7 %collective-permute-done.19 = f32[136,128]{1,0:T(8,128)S(1)} collective-permute-done((f32[136,128]{1,0:T(8,128)S(1)}, f32[136,128]{1,0:T(8,128)S(1)}, u32[]{:S(2)}, u32[]{:S(2)}) %collective-permute-start.19) | collective-permute-done | bytes 69664 | tf_op jit(solution)/shard_map/ppermute | solution.py:373
  78.9 3.7 %collective-permute-start.20 = (f32[136,128]{1,0:T(8,128)S(1)}, f32[136,128]{1,0:T(8,128)S(1)}, u32[]{:S(2)}, u32[]{:S(2)}) collective-permute-start(f32[136,128]{1,0:T(8,128)S(1)} %add.26), channel_id=1, source_target_pairs={{0,96},{8,104},{16,112},{24,120},{32,64},{40,72},{48,80},{56,88},{... | collective-permute-start | bytes 208904 | tf_op jit(solution)/shard_map/ppermute | solution.py:374
  82.6 1.7 %collective-permute-done.20 = f32[136,128]{1,0:T(8,128)S(1)} collective-permute-done((f32[136,128]{1,0:T(8,128)S(1)}, f32[136,128]{1,0:T(8,128)S(1)}, u32[]{:S(2)}, u32[]{:S(2)}) %collective-permute-start.20) | collective-permute-done | bytes 69664 | tf_op jit(solution)/shard_map/ppermute | solution.py:374
  84.4 6.9 %collective-permute-start.21 = (f32[136,128]{1,0:T(8,128)S(1)}, f32[136,128]{1,0:T(8,128)S(1)}, u32[]{:S(2)}, u32[]{:S(2)}) collective-permute-start(f32[136,128]{1,0:T(8,128)S(1)} %add.27.mine), channel_id=1, source_target_pairs={{0,1},{1,0},{2,3},{3,2},{4,5},{5,4},{6,7},{7,6},{8,9},{9,8},{10,11... | collective-permute-start | bytes 208904 | tf_op jit(solution)/shard_map/ppermute | solution.py:333
  92.2 43.2 %finish.1 = (f32[1024,256]{1,0:T(8,128)}, f32[256,256]{1,0:T(8,128)}) custom-call(f32[136,128]{1,0:T(8,128)S(1)} %add.27.mine, f32[136,128]{1,0:T(8,128)S(1)} %collective-permute-done.21.other, f32[1024,256]{1,0:T(8,128)S(1)} %get-tuple-element.41.prod), custom_call_target="tpu_custom_call" | custom-call | tf_op jit(solution)/shard_map/finish/pallas_call | solution.py:305
  (47 shorter events, 17.5 us)
Async XLA Ops:
  0.6 13.1 %slice-start = ((s8[16777216]{0:T(1024)(128)(4,1)}), s8[4194304]{0:T(1024)(128)(4,1)S(1)}, s32[]{:S(2)}) async-start(s8[16777216]{0:T(1024)(128)(4,1)} %bitcast.3), calls=%async_computation | async-start | bytes 8388608
  0.6 13.1 %slice-start.1 = ((s8[16777216]{0:T(1024)(128)(4,1)}), s8[4194304]{0:T(1024)(128)(4,1)S(1)}, s32[]{:S(2)}) async-start(s8[16777216]{0:T(1024)(128)(4,1)} %bitcast.3), calls=%async_computation.1 | async-start | bytes 8388608
  8.1 3.0 %collective-permute-start.1 = (f32[512,256]{1,0:T(8,128)S(1)}, f32[512,256]{1,0:T(8,128)S(1)}, u32[]{:S(2)}, u32[]{:S(2)}) collective-permute-start(f32[512,256]{1,0:T(8,128)S(1)} %get-tuple-element.22), channel_id=1, source_target_pairs={{0,1},{1,0},{2,3},{3,2},{4,5},{5,4},{6,7},{7,6},{8,9},{9,8},{10,11... | collective-permute-start | bytes 1572872 | tf_op jit(solution)/shard_map/ppermute | solution.py:333
  9.5 2.9 %collective-permute-start = (f32[512,256]{1,0:T(8,128)S(1)}, f32[512,256]{1,0:T(8,128)S(1)}, u32[]{:S(2)}, u32[]{:S(2)}) collective-permute-start(f32[512,256]{1,0:T(8,128)S(1)} %get-tuple-element.26), channel_id=1, source_target_pairs={{0,1},{1,0},{2,3},{3,2},{4,5},{5,4},{6,7},{7,6},{8,9},{9,8},{10,11... | collective-permute-start | bytes 1572872 | tf_op jit(solution)/shard_map/ppermute | solution.py:333
  15.4 5.5 %collective-permute-start.2 = (f32[512,256]{1,0:T(8,128)S(1)}, f32[512,256]{1,0:T(8,128)S(1)}, u32[]{:S(2)}, u32[]{:S(2)}) collective-permute-start(f32[512,256]{1,0:T(8,128)S(1)} %get-tuple-element.27.refs_0_), channel_id=1, source_target_pairs={{0,1},{1,0},{2,3},{3,2},{4,5},{5,4},{6,7},{7,6},{8,9},{9,8},{10,11... | collective-permute-start | bytes 1572872 | tf_op jit(solution)/shard_map/ppermute | solution.py:333
  15.8 5.1 %collective-permute-start.3 = (f32[512,256]{1,0:T(8,128)S(1)}, f32[512,256]{1,0:T(8,128)S(1)}, u32[]{:S(2)}, u32[]{:S(2)}) collective-permute-start(f32[512,256]{1,0:T(8,128)S(1)} %get-tuple-element.28.refs_1_), channel_id=1, source_target_pairs={{0,1},{1,0},{2,3},{3,2},{4,5},{5,4},{6,7},{7,6},{8,9},{9,8},{10,11... | collective-permute-start | bytes 1572872 | tf_op jit(solution)/shard_map/ppermute | solution.py:333
  15.9 13.5 %collective-permute-start.9 = (f32[512,256]{1,0:T(8,128)S(1)}, f32[512,256]{1,0:T(8,128)S(1)}, u32[]{:S(2)}, u32[]{:S(2)}) collective-permute-start(f32[512,256]{1,0:T(8,128)S(1)} %spmm.9.refs_0_), channel_id=1, source_target_pairs={{0,6},{1,7},{2,0},{3,1},{4,2},{5,3},{6,4},{7,5},{8,14},{9,15},{10,... | collective-permute-start | bytes 1572872 | tf_op jit(solution)/shard_map/ppermute | solution.py:333
  18.5 14.0 %collective-permute-start.8 = (f32[512,256]{1,0:T(8,128)S(1)}, f32[512,256]{1,0:T(8,128)S(1)}, u32[]{:S(2)}, u32[]{:S(2)}) collective-permute-start(f32[512,256]{1,0:T(8,128)S(1)} %spmm.8.refs_1_), channel_id=1, source_target_pairs={{0,2},{1,3},{2,4},{3,5},{4,6},{5,7},{6,0},{7,1},{8,10},{9,11},{10,... | collective-permute-start | bytes 1572872 | tf_op jit(solution)/shard_map/ppermute | solution.py:333
  20.1 12.8 %collective-permute-start.6 = (f32[512,256]{1,0:T(8,128)S(1)}, f32[512,256]{1,0:T(8,128)S(1)}, u32[]{:S(2)}, u32[]{:S(2)}) collective-permute-start(f32[512,256]{1,0:T(8,128)S(1)} %get-tuple-element.29.refs_2_), channel_id=1, source_target_pairs={{0,1},{1,0},{2,3},{3,2},{4,5},{5,4},{6,7},{7,6},{8,9},{9,8},{10,11... | collective-permute-start | bytes 1572872 | tf_op jit(solution)/shard_map/ppermute | solution.py:333
  20.8 13.6 %collective-permute-start.7 = (f32[512,256]{1,0:T(8,128)S(1)}, f32[512,256]{1,0:T(8,128)S(1)}, u32[]{:S(2)}, u32[]{:S(2)}) collective-permute-start(f32[512,256]{1,0:T(8,128)S(1)} %get-tuple-element.30.refs_3_), channel_id=1, source_target_pairs={{0,1},{1,0},{2,3},{3,2},{4,5},{5,4},{6,7},{7,6},{8,9},{9,8},{10,11... | collective-permute-start | bytes 1572872 | tf_op jit(solution)/shard_map/ppermute | solution.py:333
  24.0 13.8 %collective-permute-start.4 = (f32[512,256]{1,0:T(8,128)S(1)}, f32[512,256]{1,0:T(8,128)S(1)}, u32[]{:S(2)}, u32[]{:S(2)}) collective-permute-start(f32[512,256]{1,0:T(8,128)S(1)} %get-tuple-element.32.refs_4_), channel_id=1, source_target_pairs={{0,1},{1,0},{2,3},{3,2},{4,5},{5,4},{6,7},{7,6},{8,9},{9,8},{10,11... | collective-permute-start | bytes 1572872 | tf_op jit(solution)/shard_map/ppermute | solution.py:333
  29.4 15.1 %collective-permute-start.12 = (f32[512,256]{1,0:T(8,128)S(1)}, f32[512,256]{1,0:T(8,128)S(1)}, u32[]{:S(2)}, u32[]{:S(2)}) collective-permute-start(f32[512,256]{1,0:T(8,128)S(1)} %get-tuple-element.31.refs_0_), channel_id=1, source_target_pairs={{0,2},{1,3},{2,4},{3,5},{4,6},{5,7},{6,0},{7,1},{8,10},{9,11},{10,... | collective-permute-start | bytes 1572872 | tf_op jit(solution)/shard_map/ppermute | solution.py:333
  32.6 12.0 %collective-permute-start.11 = (f32[512,256]{1,0:T(8,128)S(1)}, f32[512,256]{1,0:T(8,128)S(1)}, u32[]{:S(2)}, u32[]{:S(2)}) collective-permute-start(f32[512,256]{1,0:T(8,128)S(1)} %get-tuple-element.37), channel_id=1, source_target_pairs={{0,6},{1,7},{2,0},{3,1},{4,2},{5,3},{6,4},{7,5},{8,14},{9,15},{10,... | collective-permute-start | bytes 1572872 | tf_op jit(solution)/shard_map/ppermute | solution.py:333
  32.9 4.9 %collective-permute-start.5 = (f32[512,256]{1,0:T(8,128)S(1)}, f32[512,256]{1,0:T(8,128)S(1)}, u32[]{:S(2)}, u32[]{:S(2)}) collective-permute-start(f32[512,256]{1,0:T(8,128)S(1)} %get-tuple-element.33.refs_5_), channel_id=1, source_target_pairs={{0,1},{1,0},{2,3},{3,2},{4,5},{5,4},{6,7},{7,6},{8,9},{9,8},{10,11... | collective-permute-start | bytes 1572872 | tf_op jit(solution)/shard_map/ppermute | solution.py:333
  35.9 19.9 %collective-permute-start.13 = (f32[512,256]{1,0:T(8,128)S(1)}, f32[512,256]{1,0:T(8,128)S(1)}, u32[]{:S(2)}, u32[]{:S(2)}) collective-permute-start(f32[512,256]{1,0:T(8,128)S(1)} %get-tuple-element.38), channel_id=1, source_target_pairs={{0,6},{1,7},{2,0},{3,1},{4,2},{5,3},{6,4},{7,5},{8,14},{9,15},{10,... | collective-permute-start | bytes 1572872 | tf_op jit(solution)/shard_map/ppermute | solution.py:333
  37.7 18.0 %collective-permute-start.10 = (f32[512,256]{1,0:T(8,128)S(1)}, f32[512,256]{1,0:T(8,128)S(1)}, u32[]{:S(2)}, u32[]{:S(2)}) collective-permute-start(f32[512,256]{1,0:T(8,128)S(1)} %get-tuple-element.34.refs_2_), channel_id=1, source_target_pairs={{0,2},{1,3},{2,4},{3,5},{4,6},{5,7},{6,0},{7,1},{8,10},{9,11},{10,... | collective-permute-start | bytes 1572872 | tf_op jit(solution)/shard_map/ppermute | solution.py:333
  56.4 3.4 %collective-permute-start.14 = (f32[136,128]{1,0:T(8,128)S(1)}, f32[136,128]{1,0:T(8,128)S(1)}, u32[]{:S(2)}, u32[]{:S(2)}) collective-permute-start(f32[136,128]{1,0:T(8,128)S(1)} %get-tuple-element.40), channel_id=1, source_target_pairs={{0,1},{1,0},{2,3},{3,2},{4,5},{5,4},{6,7},{7,6},{8,9},{9,8},{10,11... | collective-permute-start | bytes 208904 | tf_op jit(solution)/shard_map/ppermute | solution.py:333
  59.8 3.2 %collective-permute-start.15 = (f32[136,128]{1,0:T(8,128)S(1)}, f32[136,128]{1,0:T(8,128)S(1)}, u32[]{:S(2)}, u32[]{:S(2)}) collective-permute-start(f32[136,128]{1,0:T(8,128)S(1)} %add.21), channel_id=1, source_target_pairs={{0,2},{1,3},{2,0},{3,1},{4,6},{5,7},{6,4},{7,5},{8,10},{9,11},{10,... | collective-permute-start | bytes 208904 | tf_op jit(solution)/shard_map/ppermute | solution.py:372
  63.0 3.4 %collective-permute-start.16 = (f32[136,128]{1,0:T(8,128)S(1)}, f32[136,128]{1,0:T(8,128)S(1)}, u32[]{:S(2)}, u32[]{:S(2)}) collective-permute-start(f32[136,128]{1,0:T(8,128)S(1)} %add.22), channel_id=1, source_target_pairs={{0,8},{8,0},{16,24},{24,16},{32,40},{40,32},{48,56},{56,48},{64,72... | collective-permute-start | bytes 208904 | tf_op jit(solution)/shard_map/ppermute | solution.py:373
  66.5 3.4 %collective-permute-start.17 = (f32[136,128]{1,0:T(8,128)S(1)}, f32[136,128]{1,0:T(8,128)S(1)}, u32[]{:S(2)}, u32[]{:S(2)}) collective-permute-start(f32[136,128]{1,0:T(8,128)S(1)} %add.23), channel_id=1, source_target_pairs={{0,32},{8,40},{16,48},{24,56},{32,0},{40,8},{48,16},{56,24},{64,96... | collective-permute-start | bytes 208904 | tf_op jit(solution)/shard_map/ppermute | solution.py:374
  69.9 4.5 %collective-permute-start.18 = (f32[136,128]{1,0:T(8,128)S(1)}, f32[136,128]{1,0:T(8,128)S(1)}, u32[]{:S(2)}, u32[]{:S(2)}) collective-permute-start(f32[136,128]{1,0:T(8,128)S(1)} %add.24), channel_id=1, source_target_pairs={{0,6},{1,7},{2,4},{3,5},{4,2},{5,3},{6,0},{7,1},{8,14},{9,15},{10,... | collective-permute-start | bytes 208904 | tf_op jit(solution)/shard_map/ppermute | solution.py:372
  74.4 4.5 %collective-permute-start.19 = (f32[136,128]{1,0:T(8,128)S(1)}, f32[136,128]{1,0:T(8,128)S(1)}, u32[]{:S(2)}, u32[]{:S(2)}) collective-permute-start(f32[136,128]{1,0:T(8,128)S(1)} %add.25), channel_id=1, source_target_pairs={{0,24},{8,16},{16,8},{24,0},{32,56},{40,48},{48,40},{56,32},{64,88... | collective-permute-start | bytes 208904 | tf_op jit(solution)/shard_map/ppermute | solution.py:373
  78.9 5.4 %collective-permute-start.20 = (f32[136,128]{1,0:T(8,128)S(1)}, f32[136,128]{1,0:T(8,128)S(1)}, u32[]{:S(2)}, u32[]{:S(2)}) collective-permute-start(f32[136,128]{1,0:T(8,128)S(1)} %add.26), channel_id=1, source_target_pairs={{0,96},{8,104},{16,112},{24,120},{32,64},{40,72},{48,80},{56,88},{... | collective-permute-start | bytes 208904 | tf_op jit(solution)/shard_map/ppermute | solution.py:374
  84.4 7.8 %collective-permute-start.21 = (f32[136,128]{1,0:T(8,128)S(1)}, f32[136,128]{1,0:T(8,128)S(1)}, u32[]{:S(2)}, u32[]{:S(2)}) collective-permute-start(f32[136,128]{1,0:T(8,128)S(1)} %add.27.mine), channel_id=1, source_target_pairs={{0,1},{1,0},{2,3},{3,2},{4,5},{5,4},{6,7},{7,6},{8,9},{9,8},{10,11... | collective-permute-start | bytes 208904 | tf_op jit(solution)/shard_map/ppermute | solution.py:333
  (2 other events, 15.8 us)
where the time goes:
time: 136 us; the launch traced here: 135 us
  Pallas kernels  63.1 us (46%)
  waiting for transfers between devices  40 us (29%)
  starting transfers between devices  31.4 us (23%)
    pallas_call x1, Pallas kernels, finish(): pl.pallas_call(functools.partial(basis_kernel, root), in_specs=[vmem] * 3...  43.2 us
    ppermute x16, waiting for transfers between devices, move(): return lax.ppermute(q, 'col', to)  26.9 us
    ppermute x16, starting transfers between devices, move(): return lax.ppermute(q, 'col', to)  20 us
    pallas_call x8, Pallas kernels, spmm(): pl.pallas_call(functools.partial(spmm_kernel, items, len(adds), len(after...  11.8 us
    pallas_call x1, Pallas kernels, first(): pl.pallas_call(functools.partial(first_kernel, items, kept), in_specs=[sm...  7.42 us
    ppermute x2, waiting for transfers between devices, on_device(): lax.ppermute(tot, 'col', perm(8, lambda c: pair(c // 2) * 2 + c % 2))  6.02 us
    ppermute x2, starting transfers between devices, on_device(): lax.ppermute(tot, 'row', perm(16, lambda r: pair(r // 4) * 4 + r % 4))  5.4 us
    ppermute x2, starting transfers between devices, on_device(): lax.ppermute(tot, 'row', perm(16, lambda r: r // 4 * 4 + pair(r % 4)))  4.4 us
  transfers between devices with their start and end apart: 22, of which 13 were waited for; matrix products, arithmetic and copies ran while one was open for 0% of the time, Pallas kernels for 7%

commit v1 on v0

--- a/solution.py
+++ b/solution.py
@@ -34,9 +34,8 @@
     return dot(ah, bh, dims) + (dot(ah, bl, dims) + dot(al, bh, dims))
 
 
-def first_row(item):
+def first_row(me, item):
     dx, flip, half = item
-    me = lax.axis_index("col")
     return ((((me >> 1) + dx) & 3) * 2 + ((me + flip) & 1)) * 2 * RB + half * RB
 
 
@@ -45,66 +44,91 @@
     dense = []
     blocks = []
     for s in range(SLOTS):
-        scale = jnp.where(s < live, scales[s, row], 0.0)
-        dense.append((tile(s).astype(F32) * scale).astype(BF16))
+        scaled = jnp.where(s < live, tile(s).astype(F32) * scales[s, row], 0.0)
+        dense.append(scaled.astype(BF16))
         start = pl.multiple_of(cols[s, row] * T, T)
         blocks.append(sketch[pl.ds(start, T), :])
     return dot(jnp.concatenate(dense, axis=1), jnp.concatenate(blocks, axis=0))
 
 
+def tile_copies(me, items, counts, tiles, into, sem):
+    copies = []
+    for i, item in enumerate(items):
+        for r in range(RB):
+            row = first_row(me, item) + r
+            pairs = (counts[0, row] + 1) >> 1
+            at = i * RB + r
+            for p in range(1, SLOTS // 2 + 1):
+                part = pl.ds(0, 2 * p)
+                copy = pltpu.make_async_copy(tiles.at[row, part], into.at[at, part], sem.at[at])
+                copies.append((pairs == p, copy))
+    return copies
+
+
+def start_all(copies):
+    for chosen, copy in copies:
+        pl.when(chosen)(copy.start)
+
+
+def wait_all(copies):
+    for chosen, copy in copies:
+        pl.when(chosen)(copy.wait)
+
+
 def first_kernel(items, kept, cols, counts, scales, tiles, sketch, *refs):
     n = len(items)
-    outs, (held, local), (tile_sem, held_sem, sketch_sem) = refs[:n], refs[n:n + 2], refs[n + 3:]
-    buf = refs[n + 2]
+    outs, (held, local) = refs[:n], refs[n:n + 2]
+    buf, meta, meta_sem, tile_sem, held_sem, sketch_sem = (
+        refs[n + 2], refs[n + 3:n + 6], *refs[n + 6:]
+    )
+    me = lax.axis_index("col")
     piece = local.shape[0] // SKETCH_PIECES
-    load = []
+    load = [
+        pltpu.make_async_copy(src, dst, meta_sem.at[i])
+        for i, (src, dst) in enumerate(zip((cols, counts, scales), meta))
+    ]
     for j in range(SKETCH_PIECES):
         rows = pl.ds(j * piece, piece)
         load.append(pltpu.make_async_copy(sketch.at[rows], local.at[rows], sketch_sem.at[j]))
-    tile_load, held_load = [], []
-    for group, into, sem, out in ((items, buf, tile_sem, tile_load), (kept, held, held_sem, held_load)):
-        for i, item in enumerate(group):
-            for r in range(RB):
-                for p in range(2):
-                    part = pl.ds(p * (SLOTS // 2), SLOTS // 2)
-                    to = i * RB + r
-                    out.append(pltpu.make_async_copy(
-                        tiles.at[first_row(item) + r, part], into.at[to, part], sem.at[2 * to + p]
-                    ))
-    for copy in load + tile_load + held_load:
+    for copy in load:
         copy.start()
-    for copy in load:
+    for copy in load[:3]:
         copy.wait()
+    mine = tile_copies(me, items, meta[1], tiles, buf, tile_sem)
+    later = tile_copies(me, kept, meta[1], tiles, held, held_sem)
+    start_all(mine)
+    start_all(later)
+    for copy in load[3:]:
+        copy.wait()
+    wait_all(mine)
     for i, item in enumerate(items):
+        base = first_row(me, item)
         for r in range(RB):
-            to = i * RB + r
-            tile_load[2 * to].wait()
-            tile_load[2 * to + 1].wait()
             outs[i][r * T:(r + 1) * T, :] = block_row(
-                first_row(item) + r, lambda s: buf[to, s], cols, counts, scales, local
+                base + r, lambda s: buf[i * RB + r, s], *meta, local
             )
-    for copy in held_load:
-        copy.wait()
+    wait_all(later)
 
 
 def first(items, kept, meta, tiles, sketch):
     vmem = pl.BlockSpec(memory_space=pltpu.VMEM)
-    smem = pl.BlockSpec(memory_space=pltpu.SMEM)
     hbm = pl.BlockSpec(memory_space=pltpu.HBM)
     rows, keep = RB * len(items), RB * len(kept)
     return pl.pallas_call(
         functools.partial(first_kernel, items, kept),
-        in_specs=[smem] * 3 + [hbm] * 2,
+        in_specs=[hbm] * 5,
         out_specs=[vmem] * (len(items) + 2),
         out_shape=[jax.ShapeDtypeStruct((HALF, K), F32)] * len(items)
         + [
             jax.ShapeDtypeStruct((keep, SLOTS, T, T), BF16),
             jax.ShapeDtypeStruct(sketch.shape, BF16),
         ],
-        scratch_shapes=[
-            pltpu.VMEM((rows, SLOTS, T, T), BF16),
-            pltpu.SemaphoreType.DMA((2 * rows,)),
-            pltpu.SemaphoreType.DMA((2 * keep,)),
+        scratch_shapes=[pltpu.VMEM((rows, SLOTS, T, T), BF16)]
+        + [pltpu.SMEM(a.shape, a.dtype) for a in meta]
+        + [
+            pltpu.SemaphoreType.DMA((3,)),
+            pltpu.SemaphoreType.DMA((rows,)),
+            pltpu.SemaphoreType.DMA((keep,)),
             pltpu.SemaphoreType.DMA((SKETCH_PIECES,)),
         ],
         compiler_params=pltpu.CompilerParams(vmem_limit_bytes=VMEM_LIMIT),
@@ -115,35 +139,51 @@
     )(*meta, tiles, sketch)
 
 
-def spmm_kernel(items, joins, waits, held, cols, counts, scales, tiles, sketch, *refs):
-    adds = refs[:joins]
-    outs = refs[joins + waits:]
-    for n, item in enumerate(items):
-        base = first_row(item)
+def spmm_kernel(items, at, loads, joins, cols, counts, scales, tiles, sketch, *refs):
+    n = len(items)
+    me = lax.axis_index("col")
+    adds, outs = refs[:joins], refs[joins:joins + n]
+    held, copies = tiles, []
+    if loads:
+        held, sem = refs[joins + n:]
+        copies = tile_copies(me, loads, counts, tiles, held, sem)
+    start_all(copies)
+    first_ones = RB * n * (SLOTS // 2)
+    wait_all(copies[:first_ones])
+    for i, item in enumerate(items):
+        base = first_row(me, item)
         for r in range(RB):
-            at = held * RB + n * RB + r if held is not None else base + r
-            acc = block_row(base + r, lambda s: tiles[at, s], cols, counts, scales, sketch)
+            to = (at + i) * RB + r
+            acc = block_row(base + r, lambda s: held[to, s], cols, counts, scales, sketch)
             rows = slice(r * T, (r + 1) * T)
-            for j in range(n, joins, len(items)):
+            for j in range(i, joins, n):
                 acc = acc + adds[j][rows, :]
-            outs[n][rows, :] = acc
-
-
-def spmm(items, meta, tiles, sketch, adds=(), after=(), held=None):
+            outs[i][rows, :] = acc
+    wait_all(copies[first_ones:])
+
+
+def spmm(items, at, meta, tiles, sketch, adds=(), loads=()):
     vmem = pl.BlockSpec(memory_space=pltpu.VMEM)
     smem = pl.BlockSpec(memory_space=pltpu.SMEM)
-    anywhere = pl.BlockSpec(memory_space=pl.ANY)
+    hbm = pl.BlockSpec(memory_space=pltpu.HBM)
+    keep = RB * len(loads)
+    out_shape = [jax.ShapeDtypeStruct((HALF, K), F32)] * len(items)
+    scratch = []
+    if loads:
+        out_shape.append(jax.ShapeDtypeStruct((keep, SLOTS, T, T), BF16))
+        scratch.append(pltpu.SemaphoreType.DMA((keep,)))
     return pl.pallas_call(
-        functools.partial(spmm_kernel, items, len(adds), len(after), held),
-        in_specs=[smem] * 3 + [vmem] * (2 + len(adds)) + [anywhere] * len(after),
-        out_specs=[vmem] * len(items),
-        out_shape=[jax.ShapeDtypeStruct((HALF, K), F32)] * len(items),
+        functools.partial(spmm_kernel, items, at, loads, len(adds)),
+        in_specs=[smem] * 3 + [hbm if loads else vmem, vmem] + [vmem] * len(adds),
+        out_specs=[vmem] * len(out_shape),
+        out_shape=out_shape,
+        scratch_shapes=scratch,
         compiler_params=pltpu.CompilerParams(vmem_limit_bytes=VMEM_LIMIT),
         cost_estimate=pl.CostEstimate(
             flops=2 * len(items) * HALF * SLOTS * T * K, bytes_accessed=4 << 20, transcendentals=0
         ),
         name="spmm",
-    )(*meta, tiles, sketch, *adds, *after)
+    )(*meta, tiles, sketch, *adds)
 
 
 PACK = 272
@@ -316,8 +356,21 @@
     )(mine, other, prod)
 
 
+ORDERS = ((2, 1), (1, 0), (0, 2))
+
+
 def perm(size, target):
     return [(i, target(i)) for i in range(size)]
+
+
+def axis_perm(order, by):
+    def target(i):
+        place = [i >> 5, (i >> 3) & 3, (i >> 1) & 3]
+        axis = order[i & 1]
+        place[axis] = (place[axis] + by) & 3
+        return (((place[0] * 4 + place[1]) * 4 + place[2]) << 1) | (i & 1)
+
+    return perm(128, target)
 
 
 def on_device(tiles, tile_cols, counts, scales, sketch):
@@ -332,46 +385,41 @@
     def move(q, to):
         return lax.ppermute(q, "col", to)
 
-    qa, qb, held, local = first(
-        ((2, 1, 0), (2, 1, 1)),
-        ((2, 0, 0), (2, 0, 1)),
-        meta,
-        pltpu.with_memory_space_constraint(tiles, pltpu.HBM),
-        pltpu.with_memory_space_constraint(sketch, pltpu.HBM),
-    )
-    later, _ = lax.optimization_barrier((tiles, qa))
-    near = pltpu.with_memory_space_constraint(later, pltpu.VMEM)
-
-    def sp(*items, tiles=near, **kw):
-        return spmm(items, meta, tiles, local, **kw)
+    far_other = (2, 1, 0), (2, 1, 1)
+    far_own = (2, 0, 0), (2, 0, 1)
+    u_other, u_own = ((1, 1, 1), (3, 1, 0)), ((1, 0, 1), (3, 0, 0))
+    v_other, v_own = ((1, 1, 0), (3, 1, 1)), ((1, 0, 0), (3, 0, 1))
+    here_other, here_own = ((0, 1, 0), (0, 1, 1)), ((0, 0, 0), (0, 0, 1))
+    tiles = pltpu.with_memory_space_constraint(tiles, pltpu.HBM)
+    sketch = pltpu.with_memory_space_constraint(sketch, pltpu.HBM)
+
+    qa, qb, held, local = first(far_other, far_own, meta, tiles, sketch)
+
+    def sp(items, at, held, **kw):
+        return spmm(items, at, meta, held, local, **kw)
 
     ca, cb = move(qa, partner), move(qb, partner)
-    (d2p,) = sp((2, 0, 0), tiles=held, held=0, adds=(ca,))
-    tp = move(d2p, plus)
-    (d2m,) = sp((2, 0, 1), tiles=held, held=1, adds=(cb,), after=(d2p,))
-    tm = move(d2m, minus)
-    qu = sp((1, 1, 1), (3, 1, 0), after=(d2m,))
+    d2p, d2m = sp(far_own, 0, held, adds=(ca, cb))
+    tp, tm = move(d2p, plus), move(d2m, minus)
+    rest = u_other + v_other + u_own + here_other + v_own + here_own
+    *qu, held = sp(u_other, 0, tiles, loads=rest)
     cu = [move(q, partner) for q in qu]
-    qv = sp((1, 1, 0), (3, 1, 1), after=qu)
+    qv = sp(v_other, 2, held)
     cv = [move(q, partner) for q in qv]
-    up, um = sp((1, 0, 1), (3, 0, 0), adds=cu, after=qv)
-    mid = up
+    up, um = sp(u_own, 4, held, adds=cu)
     up, um = move(up, plus), move(um, minus)
-    qo = sp((0, 1, 0), (0, 1, 1), after=(mid,))
+    qo = sp(here_other, 6, held)
     co = [move(q, partner) for q in qo]
-    vp, vm = sp((1, 0, 0), (3, 0, 1), adds=(*cv, tp, tm), after=qo)
-    last = vp
+    vp, vm = sp(v_own, 8, held, adds=(*cv, tp, tm))
     vp, vm = move(vp, plus), move(vm, minus)
-    s0, s1 = sp((0, 0, 0), (0, 0, 1), adds=co, after=(last,))
+    s0, s1 = sp(here_own, 10, held, adds=co)
 
     prod, keep, send = gram(s0, s1, vp, um, up, vm)
     tot = keep + move(send, partner)
-    even = lambda v: v ^ 1
-    odd = lambda v: (v + (1 if v % 2 else 3)) % 4
-    for pair in (even, odd):
-        tot = tot + lax.ppermute(tot, "col", perm(8, lambda c: pair(c // 2) * 2 + c % 2))
-        tot = tot + lax.ppermute(tot, "row", perm(16, lambda r: r // 4 * 4 + pair(r % 4)))
-        tot = tot + lax.ppermute(tot, "row", perm(16, lambda r: pair(r // 4) * 4 + r % 4))
+    both = ("row", "col")
+    for order in ORDERS:
+        got = [lax.ppermute(tot, both, axis_perm(order, by)) for by in (2, 3, 1)]
+        tot = (tot + got[0]) + (got[1] + got[2])
     rest = move(tot, partner)
     basis, rfac = finish(float(rows_all) ** 0.5, tot, rest, prod)
     return basis, rfac

time: 136 us -> 132 us (0.971)
  waiting for transfers between devices: 40 us -> 38.4 us
  Pallas kernels: 63.1 us -> 61.6 us
    ppermute x16, starting transfers between devices: 20 us -> 18.2 us  [move(): return lax.ppermute(q, 'col', to)]
    ppermute x6 -> x9, waiting for transfers between devices: 13 us -> 11.3 us  [on_device(): got = [lax.ppermute(tot, both, axis_perm(order, by)) for by in (2, 3, 1)]]
    pallas_call x9 -> x8, Pallas kernels: 19.3 us -> 17.8 us  [the longest x7 13.6 us: spmm(): pl.pallas_call(functools.partial(spmm_kernel, items, at, loads, len(adds)...]
    ppermute x6 -> x9, starting transfers between devices: 11.5 us -> 12.7 us  [on_device(): got = [lax.ppermute(tot, both, axis_perm(order, by)) for by in (2, 3, 1)]]
  transfers between devices with their start and end apart: 22 -> 25, of which waited for: 13 -> 13; matrix products, arithmetic and copies ran while one was open for 0% -> 0% of each run, Pallas kernels for 7% -> 10%
where the time goes in v1:
time: 132 us
  Pallas kernels  61.6 us (47%)
  waiting for transfers between devices  38.4 us (29%)
  starting transfers between devices  30.8 us (23%)
    pallas_call x1, Pallas kernels, finish(): pl.pallas_call(functools.partial(basis_kernel, root), in_specs=[vmem] * 3...  43.2 us
    ppermute x16, waiting for transfers between devices, move(): return lax.ppermute(q, 'col', to)  27.1 us
    ppermute x16, starting transfers between devices, move(): return lax.ppermute(q, 'col', to)  18.2 us
    pallas_call x7, Pallas kernels, spmm(): pl.pallas_call(functools.partial(spmm_kernel, items, at, loads, len(adds)...  13.6 us
    ppermute x9, starting transfers between devices, on_device(): got = [lax.ppermute(tot, both, axis_perm(order, by)) for by in (2, 3, 1)]  12.7 us
    ppermute x9, waiting for transfers between devices, on_device(): got = [lax.ppermute(tot, both, axis_perm(order, by)) for by in (2, 3, 1)]  11.3 us
    pallas_call x1, Pallas kernels, first(): pl.pallas_call(functools.partial(first_kernel, items, kept), in_specs=[hb...  4.13 us
  transfers between devices with their start and end apart: 25, of which 13 were waited for; matrix products, arithmetic and copies ran while one was open for 0% of the time, Pallas kernels for 10%

profile of v1, /device:TPU:1, one launch (start us, length us, event | category | flops | bytes accessed | tf_op | source)
XLA Modules:
  0.0 131.6 jit_solution(13822950454368292949)
XLA Ops:
  0.6 4.1 %first.1 = (f32[512,256]{1,0:T(8,128)S(1)}, f32[512,256]{1,0:T(8,128)S(1)}, bf16[8,8,128,128]{3,2,1,0:T(8,128)(2,1)S(1)}, bf16[8192,256]{1,0:T(8,128)(2,1)S(1)}) custom-call(s32[8,64]{1,0:T(8,128)} %bitcast.3, s32[1,64]{1,0:T(1,128)} %bitcast.19, f32[8,64]{1,0:T(8,128)} %bitcast.11, bf16[64,8,128,128]{3,2,1,0:T(8,128)(2,1)} %tiles.3, bf16[8192,256]{1,0:T(8,128)(2,1)} %sketch.1), custom_call_target="tpu_custom_call" | custom-call | flops 536870912 | bytes 8388608 | tf_op jit(solution)/shard_map/first/pallas_call | solution.py:117
  6.1 4.5 %spmm.7 = (f32[512,256]{1,0:T(8,128)S(1)}, f32[512,256]{1,0:T(8,128)S(1)}, bf16[48,8,128,128]{3,2,1,0:T(8,128)(2,1)S(1)}) custom-call(s32[8,64]{1,0:T(8,128)} %bitcast.4, s32[1,64]{1,0:T(1,128)} %bitcast.20, f32[8,64]{1,0:T(8,128)} %bitcast.12, bf16[64,8,128,128]{3,2,1,0:T(8,128)(2,1)} %tiles.3, bf16[8192,256]{1,0:T(8,128)(2,1)S(1)} %get-tuple-element.24.sketch), custom_call_target="tpu_custom_call" | custom-call | flops 536870912 | bytes 4194304 | tf_op jit(solution)/shard_map/spmm/pallas_call | solution.py:175
  13.3 1.5 %spmm.11 = (f32[512,256]{1,0:T(8,128)S(1)}, f32[512,256]{1,0:T(8,128)S(1)}) custom-call(s32[8,64]{1,0:T(8,128)} %bitcast.6, s32[1,64]{1,0:T(1,128)} %bitcast.22, f32[8,64]{1,0:T(8,128)} %bitcast.14, bf16[8,8,128,128]{3,2,1,0:T(8,128)(2,1)S(1)} %get-tuple-element.32.tiles, bf16[8192,256]{1,0:T(8,128)(2,1)S(1)} %get-tuple-element.24.sketch, ...), custom_call_target="tpu_custom_call" | custom-call | flops 536870912 | bytes 4194304 | tf_op jit(solution)/shard_map/spmm/pallas_call | solution.py:175
  16.3 1.7 %collective-permute-start.7 = (f32[512,256]{1,0:T(8,128)S(1)}, f32[512,256]{1,0:T(8,128)S(1)}, u32[]{:S(2)}, u32[]{:S(2)}) collective-permute-start(f32[512,256]{1,0:T(8,128)S(1)} %get-tuple-element.36), channel_id=1, source_target_pairs={{0,6},{1,7},{2,0},{3,1},{4,2},{5,3},{6,4},{7,5},{8,14},{9,15},{10,... | collective-permute-start | bytes 1572872 | tf_op jit(solution)/shard_map/ppermute | solution.py:386
  20.2 1.5 %spmm.13 = (f32[512,256]{1,0:T(8,128)S(1)}, f32[512,256]{1,0:T(8,128)S(1)}) custom-call(s32[8,64]{1,0:T(8,128)} %bitcast.8, s32[1,64]{1,0:T(1,128)} %bitcast.24, f32[8,64]{1,0:T(8,128)} %bitcast.16, bf16[48,8,128,128]{3,2,1,0:T(8,128)(2,1)S(1)} %get-tuple-element.25.tiles, bf16[8192,256]{1,0:T(8,128)(2,1)S(1)} %get-tuple-element.24.sketch, ...), custom_call_target="tpu_custom_call" | custom-call | flops 536870912 | bytes 4194304 | tf_op jit(solution)/shard_map/spmm/pallas_call | solution.py:175
  21.9 1.7 %collective-permute-start.11 = (f32[512,256]{1,0:T(8,128)S(1)}, f32[512,256]{1,0:T(8,128)S(1)}, u32[]{:S(2)}, u32[]{:S(2)}) collective-permute-start(f32[512,256]{1,0:T(8,128)S(1)} %get-tuple-element.40), channel_id=1, source_target_pairs={{0,6},{1,7},{2,0},{3,1},{4,2},{5,3},{6,4},{7,5},{8,14},{9,15},{10,... | collective-permute-start | bytes 1572872 | tf_op jit(solution)/shard_map/ppermute | solution.py:386
  23.6 6.2 %collective-permute-done.6.refs_2_ = f32[512,256]{1,0:T(8,128)S(1)} collective-permute-done((f32[512,256]{1,0:T(8,128)S(1)}, f32[512,256]{1,0:T(8,128)S(1)}, u32[]{:S(2)}, u32[]{:S(2)}) %collective-permute-start.6) | collective-permute-done | bytes 524320 | tf_op jit(solution)/shard_map/ppermute | solution.py:386
  29.8 1.6 %spmm.12 = (f32[512,256]{1,0:T(8,128)S(1)}, f32[512,256]{1,0:T(8,128)S(1)}) custom-call(s32[8,64]{1,0:T(8,128)} %bitcast.9, s32[1,64]{1,0:T(1,128)} %bitcast.25, f32[8,64]{1,0:T(8,128)} %bitcast.17, bf16[48,8,128,128]{3,2,1,0:T(8,128)(2,1)S(1)} %get-tuple-element.25.tiles, bf16[8192,256]{1,0:T(8,128)(2,1)S(1)} %get-tuple-element.24.sketch, ...), custom_call_target="tpu_custom_call" | custom-call | flops 536870912 | bytes 4194304 | tf_op jit(solution)/shard_map/spmm/pallas_call | solution.py:175
  32.6 1.6 %collective-permute-start.13 = (f32[512,256]{1,0:T(8,128)S(1)}, f32[512,256]{1,0:T(8,128)S(1)}, u32[]{:S(2)}, u32[]{:S(2)}) collective-permute-start(f32[512,256]{1,0:T(8,128)S(1)} %get-tuple-element.42), channel_id=1, source_target_pairs={{0,6},{1,7},{2,0},{3,1},{4,2},{5,3},{6,4},{7,5},{8,14},{9,15},{10,... | collective-permute-start | bytes 1572872 | tf_op jit(solution)/shard_map/ppermute | solution.py:386
  34.2 1.5 %spmm.9 = (f32[512,256]{1,0:T(8,128)S(1)}, f32[512,256]{1,0:T(8,128)S(1)}) custom-call(s32[8,64]{1,0:T(8,128)} %bitcast.10, s32[1,64]{1,0:T(1,128)} %bitcast.26, f32[8,64]{1,0:T(8,128)} %bitcast.18, bf16[48,8,128,128]{3,2,1,0:T(8,128)(2,1)S(1)} %get-tuple-element.25.tiles, bf16[8192,256]{1,0:T(8,128)(2,1)S(1)} %get-tuple-element.24.sketch, ...), custom_call_target="tpu_custom_call" | custom-call | flops 536870912 | bytes 4194304 | tf_op jit(solution)/shard_map/spmm/pallas_call | solution.py:175
  35.8 4.6 %collective-permute-done.11.um = f32[512,256]{1,0:T(8,128)S(1)} collective-permute-done((f32[512,256]{1,0:T(8,128)S(1)}, f32[512,256]{1,0:T(8,128)S(1)}, u32[]{:S(2)}, u32[]{:S(2)}) %collective-permute-start.11) | collective-permute-done | bytes 524320 | tf_op jit(solution)/shard_map/ppermute | solution.py:386
  40.4 3.2 %collective-permute-done.12.up = f32[512,256]{1,0:T(8,128)S(1)} collective-permute-done((f32[512,256]{1,0:T(8,128)S(1)}, f32[512,256]{1,0:T(8,128)S(1)}, u32[]{:S(2)}, u32[]{:S(2)}) %collective-permute-start.12) | collective-permute-done | bytes 524320 | tf_op jit(solution)/shard_map/ppermute | solution.py:386
  43.6 11.2 %collective-permute-done.8.vp = f32[512,256]{1,0:T(8,128)S(1)} collective-permute-done((f32[512,256]{1,0:T(8,128)S(1)}, f32[512,256]{1,0:T(8,128)S(1)}, u32[]{:S(2)}, u32[]{:S(2)}) %collective-permute-start.8) | collective-permute-done | bytes 524320 | tf_op jit(solution)/shard_map/ppermute | solution.py:386
  55.4 1.9 %collective-permute-start.14 = (f32[136,128]{1,0:T(8,128)S(1)}, f32[136,128]{1,0:T(8,128)S(1)}, u32[]{:S(2)}, u32[]{:S(2)}) collective-permute-start(f32[136,128]{1,0:T(8,128)S(1)} %get-tuple-element.44), channel_id=1, source_target_pairs={{0,1},{1,0},{2,3},{3,2},{4,5},{5,4},{6,7},{7,6},{8,9},{9,8},{10,11... | collective-permute-start | bytes 208904 | tf_op jit(solution)/shard_map/ppermute | solution.py:386
  58.2 1.6 %collective-permute-start.17 = (f32[136,128]{1,0:T(8,128)S(1)}, f32[136,128]{1,0:T(8,128)S(1)}, u32[]{:S(2)}, u32[]{:S(2)}) collective-permute-start(f32[136,128]{1,0:T(8,128)S(1)} %add.30), channel_id=1, source_target_pairs={{0,2},{1,9},{2,4},{3,11},{4,6},{5,13},{6,0},{7,15},{8,10},{9,17},{... | collective-permute-start | bytes 208904 | tf_op jit(solution)/shard_map/ppermute | solution.py:421
  63.3 2.7 %collective-permute-done.15 = f32[136,128]{1,0:T(8,128)S(1)} collective-permute-done((f32[136,128]{1,0:T(8,128)S(1)}, f32[136,128]{1,0:T(8,128)S(1)}, u32[]{:S(2)}, u32[]{:S(2)}) %collective-permute-start.15) | collective-permute-done | bytes 69664 | tf_op jit(solution)/shard_map/ppermute | solution.py:421
  66.0 2.0 %collective-permute-start.20 = (f32[136,128]{1,0:T(8,128)S(1)}, f32[136,128]{1,0:T(8,128)S(1)}, u32[]{:S(2)}, u32[]{:S(2)}) collective-permute-start(f32[136,128]{1,0:T(8,128)S(1)} %add_add_fusion.2), channel_id=1, source_target_pairs={{0,8},{1,33},{2,10},{3,35},{4,12},{5,37},{6,14},{7,39},{8,16},{9,4... | collective-permute-start | bytes 208904 | tf_op jit(solution)/shard_map/ppermute | solution.py:421
  68.0 2.2 %collective-permute-start.19 = (f32[136,128]{1,0:T(8,128)S(1)}, f32[136,128]{1,0:T(8,128)S(1)}, u32[]{:S(2)}, u32[]{:S(2)}) collective-permute-start(f32[136,128]{1,0:T(8,128)S(1)} %add_add_fusion.2), channel_id=1, source_target_pairs={{0,24},{1,97},{2,26},{3,99},{4,28},{5,101},{6,30},{7,103},{8,0},{9... | collective-permute-start | bytes 208904 | tf_op jit(solution)/shard_map/ppermute | solution.py:421
  71.7 3.0 %collective-permute-done.18 = f32[136,128]{1,0:T(8,128)S(1)} collective-permute-done((f32[136,128]{1,0:T(8,128)S(1)}, f32[136,128]{1,0:T(8,128)S(1)}, u32[]{:S(2)}, u32[]{:S(2)}) %collective-permute-start.18) | collective-permute-done | bytes 69664 | tf_op jit(solution)/shard_map/ppermute | solution.py:421
  74.9 2.7 %collective-permute-start.22 = (f32[136,128]{1,0:T(8,128)S(1)}, f32[136,128]{1,0:T(8,128)S(1)}, u32[]{:S(2)}, u32[]{:S(2)}) collective-permute-start(f32[136,128]{1,0:T(8,128)S(1)} %add_add_fusion.1), channel_id=1, source_target_pairs={{0,96},{1,7},{2,98},{3,1},{4,100},{5,3},{6,102},{7,5},{8,104},{9,1... | collective-permute-start | bytes 208904 | tf_op jit(solution)/shard_map/ppermute | solution.py:421
  77.6 1.7 %collective-permute-done.23 = f32[136,128]{1,0:T(8,128)S(1)} collective-permute-done((f32[136,128]{1,0:T(8,128)S(1)}, f32[136,128]{1,0:T(8,128)S(1)}, u32[]{:S(2)}, u32[]{:S(2)}) %collective-permute-start.23) | collective-permute-done | bytes 69664 | tf_op jit(solution)/shard_map/ppermute | solution.py:421
  79.6 2.7 %collective-permute-done.21 = f32[136,128]{1,0:T(8,128)S(1)} collective-permute-done((f32[136,128]{1,0:T(8,128)S(1)}, f32[136,128]{1,0:T(8,128)S(1)}, u32[]{:S(2)}, u32[]{:S(2)}) %collective-permute-start.21) | collective-permute-done | bytes 69664 | tf_op jit(solution)/shard_map/ppermute | solution.py:421
  82.2 5.3 %collective-permute-start.24 = (f32[136,128]{1,0:T(8,128)S(1)}, f32[136,128]{1,0:T(8,128)S(1)}, u32[]{:S(2)}, u32[]{:S(2)}) collective-permute-start(f32[136,128]{1,0:T(8,128)S(1)} %add_add_fusion.mine), channel_id=1, source_target_pairs={{0,1},{1,0},{2,3},{3,2},{4,5},{5,4},{6,7},{7,6},{8,9},{9,8},{10,11... | collective-permute-start | bytes 208904 | tf_op jit(solution)/shard_map/ppermute | solution.py:386
  88.4 43.2 %finish.1 = (f32[1024,256]{1,0:T(8,128)}, f32[256,256]{1,0:T(8,128)}) custom-call(f32[136,128]{1,0:T(8,128)S(1)} %add_add_fusion.mine, f32[136,128]{1,0:T(8,128)S(1)} %collective-permute-done.24.other, f32[1024,256]{1,0:T(8,128)S(1)} %get-tuple-element.45.prod), custom_call_target="tpu_custom_call" | custom-call | tf_op jit(solution)/shard_map/finish/pallas_call | solution.py:345
  (40 shorter events, 16.9 us)
Async XLA Ops:
  4.8 8.4 %collective-permute-start.4 = (f32[512,256]{1,0:T(8,128)S(1)}, f32[512,256]{1,0:T(8,128)S(1)}, u32[]{:S(2)}, u32[]{:S(2)}) collective-permute-start(f32[512,256]{1,0:T(8,128)S(1)} %get-tuple-element.33), channel_id=1, source_target_pairs={{0,1},{1,0},{2,3},{3,2},{4,5},{5,4},{6,7},{7,6},{8,9},{9,8},{10,11... | collective-permute-start | bytes 1572872 | tf_op jit(solution)/shard_map/ppermute | solution.py:386
  6.1 7.3 %collective-permute-start.5 = (f32[512,256]{1,0:T(8,128)S(1)}, f32[512,256]{1,0:T(8,128)S(1)}, u32[]{:S(2)}, u32[]{:S(2)}) collective-permute-start(f32[512,256]{1,0:T(8,128)S(1)} %get-tuple-element.34), channel_id=1, source_target_pairs={{0,1},{1,0},{2,3},{3,2},{4,5},{5,4},{6,7},{7,6},{8,9},{9,8},{10,11... | collective-permute-start | bytes 1572872 | tf_op jit(solution)/shard_map/ppermute | solution.py:386
  10.6 5.6 %collective-permute-start.9 = (f32[512,256]{1,0:T(8,128)S(1)}, f32[512,256]{1,0:T(8,128)S(1)}, u32[]{:S(2)}, u32[]{:S(2)}) collective-permute-start(f32[512,256]{1,0:T(8,128)S(1)} %get-tuple-element.38), channel_id=1, source_target_pairs={{0,1},{1,0},{2,3},{3,2},{4,5},{5,4},{6,7},{7,6},{8,9},{9,8},{10,11... | collective-permute-start | bytes 1572872 | tf_op jit(solution)/shard_map/ppermute | solution.py:386
  11.1 8.5 %collective-permute-start.10 = (f32[512,256]{1,0:T(8,128)S(1)}, f32[512,256]{1,0:T(8,128)S(1)}, u32[]{:S(2)}, u32[]{:S(2)}) collective-permute-start(f32[512,256]{1,0:T(8,128)S(1)} %get-tuple-element.39), channel_id=1, source_target_pairs={{0,1},{1,0},{2,3},{3,2},{4,5},{5,4},{6,7},{7,6},{8,9},{9,8},{10,11... | collective-permute-start | bytes 1572872 | tf_op jit(solution)/shard_map/ppermute | solution.py:386
  12.7 9.0 %collective-permute-start.2 = (f32[512,256]{1,0:T(8,128)S(1)}, f32[512,256]{1,0:T(8,128)S(1)}, u32[]{:S(2)}, u32[]{:S(2)}) collective-permute-start(f32[512,256]{1,0:T(8,128)S(1)} %get-tuple-element.30), channel_id=1, source_target_pairs={{0,1},{1,0},{2,3},{3,2},{4,5},{5,4},{6,7},{7,6},{8,9},{9,8},{10,11... | collective-permute-start | bytes 1572872 | tf_op jit(solution)/shard_map/ppermute | solution.py:386
  13.2 8.7 %collective-permute-start.3 = (f32[512,256]{1,0:T(8,128)S(1)}, f32[512,256]{1,0:T(8,128)S(1)}, u32[]{:S(2)}, u32[]{:S(2)}) collective-permute-start(f32[512,256]{1,0:T(8,128)S(1)} %get-tuple-element.31), channel_id=1, source_target_pairs={{0,1},{1,0},{2,3},{3,2},{4,5},{5,4},{6,7},{7,6},{8,9},{9,8},{10,11... | collective-permute-start | bytes 1572872 | tf_op jit(solution)/shard_map/ppermute | solution.py:386
  14.9 15.0 %collective-permute-start.6 = (f32[512,256]{1,0:T(8,128)S(1)}, f32[512,256]{1,0:T(8,128)S(1)}, u32[]{:S(2)}, u32[]{:S(2)}) collective-permute-start(f32[512,256]{1,0:T(8,128)S(1)} %get-tuple-element.35), channel_id=1, source_target_pairs={{0,2},{1,3},{2,4},{3,5},{4,6},{5,7},{6,0},{7,1},{8,10},{9,11},{10,... | collective-permute-start | bytes 1572872 | tf_op jit(solution)/shard_map/ppermute | solution.py:386
  16.3 13.6 %collective-permute-start.7 = (f32[512,256]{1,0:T(8,128)S(1)}, f32[512,256]{1,0:T(8,128)S(1)}, u32[]{:S(2)}, u32[]{:S(2)}) collective-permute-start(f32[512,256]{1,0:T(8,128)S(1)} %get-tuple-element.36), channel_id=1, source_target_pairs={{0,6},{1,7},{2,0},{3,1},{4,2},{5,3},{6,4},{7,5},{8,14},{9,15},{10,... | collective-permute-start | bytes 1572872 | tf_op jit(solution)/shard_map/ppermute | solution.py:386
  19.5 13.1 %collective-permute-start = (f32[512,256]{1,0:T(8,128)S(1)}, f32[512,256]{1,0:T(8,128)S(1)}, u32[]{:S(2)}, u32[]{:S(2)}) collective-permute-start(f32[512,256]{1,0:T(8,128)S(1)} %get-tuple-element.26), channel_id=1, source_target_pairs={{0,1},{1,0},{2,3},{3,2},{4,5},{5,4},{6,7},{7,6},{8,9},{9,8},{10,11... | collective-permute-start | bytes 1572872 | tf_op jit(solution)/shard_map/ppermute | solution.py:386
  21.8 12.5 %collective-permute-start.1 = (f32[512,256]{1,0:T(8,128)S(1)}, f32[512,256]{1,0:T(8,128)S(1)}, u32[]{:S(2)}, u32[]{:S(2)}) collective-permute-start(f32[512,256]{1,0:T(8,128)S(1)} %get-tuple-element.27), channel_id=1, source_target_pairs={{0,1},{1,0},{2,3},{3,2},{4,5},{5,4},{6,7},{7,6},{8,9},{9,8},{10,11... | collective-permute-start | bytes 1572872 | tf_op jit(solution)/shard_map/ppermute | solution.py:386
  21.9 18.5 %collective-permute-start.11 = (f32[512,256]{1,0:T(8,128)S(1)}, f32[512,256]{1,0:T(8,128)S(1)}, u32[]{:S(2)}, u32[]{:S(2)}) collective-permute-start(f32[512,256]{1,0:T(8,128)S(1)} %get-tuple-element.40), channel_id=1, source_target_pairs={{0,6},{1,7},{2,0},{3,1},{4,2},{5,3},{6,4},{7,5},{8,14},{9,15},{10,... | collective-permute-start | bytes 1572872 | tf_op jit(solution)/shard_map/ppermute | solution.py:386
  29.8 13.8 %collective-permute-start.12 = (f32[512,256]{1,0:T(8,128)S(1)}, f32[512,256]{1,0:T(8,128)S(1)}, u32[]{:S(2)}, u32[]{:S(2)}) collective-permute-start(f32[512,256]{1,0:T(8,128)S(1)} %get-tuple-element.41), channel_id=1, source_target_pairs={{0,2},{1,3},{2,4},{3,5},{4,6},{5,7},{6,0},{7,1},{8,10},{9,11},{10,... | collective-permute-start | bytes 1572872 | tf_op jit(solution)/shard_map/ppermute | solution.py:386
  31.4 23.4 %collective-permute-start.8 = (f32[512,256]{1,0:T(8,128)S(1)}, f32[512,256]{1,0:T(8,128)S(1)}, u32[]{:S(2)}, u32[]{:S(2)}) collective-permute-start(f32[512,256]{1,0:T(8,128)S(1)} %get-tuple-element.37), channel_id=1, source_target_pairs={{0,2},{1,3},{2,4},{3,5},{4,6},{5,7},{6,0},{7,1},{8,10},{9,11},{10,... | collective-permute-start | bytes 1572872 | tf_op jit(solution)/shard_map/ppermute | solution.py:386
  32.6 22.2 %collective-permute-start.13 = (f32[512,256]{1,0:T(8,128)S(1)}, f32[512,256]{1,0:T(8,128)S(1)}, u32[]{:S(2)}, u32[]{:S(2)}) collective-permute-start(f32[512,256]{1,0:T(8,128)S(1)} %get-tuple-element.42), channel_id=1, source_target_pairs={{0,6},{1,7},{2,0},{3,1},{4,2},{5,3},{6,4},{7,5},{8,14},{9,15},{10,... | collective-permute-start | bytes 1572872 | tf_op jit(solution)/shard_map/ppermute | solution.py:386
  58.2 5.0 %collective-permute-start.17 = (f32[136,128]{1,0:T(8,128)S(1)}, f32[136,128]{1,0:T(8,128)S(1)}, u32[]{:S(2)}, u32[]{:S(2)}) collective-permute-start(f32[136,128]{1,0:T(8,128)S(1)} %add.30), channel_id=1, source_target_pairs={{0,2},{1,9},{2,4},{3,11},{4,6},{5,13},{6,0},{7,15},{8,10},{9,17},{... | collective-permute-start | bytes 208904 | tf_op jit(solution)/shard_map/ppermute | solution.py:421
  59.8 3.5 %collective-permute-start.16 = (f32[136,128]{1,0:T(8,128)S(1)}, f32[136,128]{1,0:T(8,128)S(1)}, u32[]{:S(2)}, u32[]{:S(2)}) collective-permute-start(f32[136,128]{1,0:T(8,128)S(1)} %add.30), channel_id=1, source_target_pairs={{0,6},{1,25},{2,0},{3,27},{4,2},{5,29},{6,4},{7,31},{8,14},{9,1},{... | collective-permute-start | bytes 208904 | tf_op jit(solution)/shard_map/ppermute | solution.py:421
  61.3 4.7 %collective-permute-start.15 = (f32[136,128]{1,0:T(8,128)S(1)}, f32[136,128]{1,0:T(8,128)S(1)}, u32[]{:S(2)}, u32[]{:S(2)}) collective-permute-start(f32[136,128]{1,0:T(8,128)S(1)} %add.30), channel_id=1, source_target_pairs={{0,4},{1,17},{2,6},{3,19},{4,0},{5,21},{6,2},{7,23},{8,12},{9,25},... | collective-permute-start | bytes 208904 | tf_op jit(solution)/shard_map/ppermute | solution.py:421
  66.0 5.8 %collective-permute-start.20 = (f32[136,128]{1,0:T(8,128)S(1)}, f32[136,128]{1,0:T(8,128)S(1)}, u32[]{:S(2)}, u32[]{:S(2)}) collective-permute-start(f32[136,128]{1,0:T(8,128)S(1)} %add_add_fusion.2), channel_id=1, source_target_pairs={{0,8},{1,33},{2,10},{3,35},{4,12},{5,37},{6,14},{7,39},{8,16},{9,4... | collective-permute-start | bytes 208904 | tf_op jit(solution)/shard_map/ppermute | solution.py:421
  68.0 3.8 %collective-permute-start.19 = (f32[136,128]{1,0:T(8,128)S(1)}, f32[136,128]{1,0:T(8,128)S(1)}, u32[]{:S(2)}, u32[]{:S(2)}) collective-permute-start(f32[136,128]{1,0:T(8,128)S(1)} %add_add_fusion.2), channel_id=1, source_target_pairs={{0,24},{1,97},{2,26},{3,99},{4,28},{5,101},{6,30},{7,103},{8,0},{9... | collective-permute-start | bytes 208904 | tf_op jit(solution)/shard_map/ppermute | solution.py:421
  70.1 4.7 %collective-permute-start.18 = (f32[136,128]{1,0:T(8,128)S(1)}, f32[136,128]{1,0:T(8,128)S(1)}, u32[]{:S(2)}, u32[]{:S(2)}) collective-permute-start(f32[136,128]{1,0:T(8,128)S(1)} %add_add_fusion.2), channel_id=1, source_target_pairs={{0,16},{1,65},{2,18},{3,67},{4,20},{5,69},{6,22},{7,71},{8,24},{9,... | collective-permute-start | bytes 208904 | tf_op jit(solution)/shard_map/ppermute | solution.py:421
  74.8 4.4 %collective-permute-start.23 = (f32[136,128]{1,0:T(8,128)S(1)}, f32[136,128]{1,0:T(8,128)S(1)}, u32[]{:S(2)}, u32[]{:S(2)}) collective-permute-start(f32[136,128]{1,0:T(8,128)S(1)} %add_add_fusion.1), channel_id=1, source_target_pairs={{0,32},{1,3},{2,34},{3,5},{4,36},{5,7},{6,38},{7,1},{8,40},{9,11},... | collective-permute-start | bytes 208904 | tf_op jit(solution)/shard_map/ppermute | solution.py:421
  74.9 4.7 %collective-permute-start.22 = (f32[136,128]{1,0:T(8,128)S(1)}, f32[136,128]{1,0:T(8,128)S(1)}, u32[]{:S(2)}, u32[]{:S(2)}) collective-permute-start(f32[136,128]{1,0:T(8,128)S(1)} %add_add_fusion.1), channel_id=1, source_target_pairs={{0,96},{1,7},{2,98},{3,1},{4,100},{5,3},{6,102},{7,5},{8,104},{9,1... | collective-permute-start | bytes 208904 | tf_op jit(solution)/shard_map/ppermute | solution.py:421
  77.6 4.7 %collective-permute-start.21 = (f32[136,128]{1,0:T(8,128)S(1)}, f32[136,128]{1,0:T(8,128)S(1)}, u32[]{:S(2)}, u32[]{:S(2)}) collective-permute-start(f32[136,128]{1,0:T(8,128)S(1)} %add_add_fusion.1), channel_id=1, source_target_pairs={{0,64},{1,5},{2,66},{3,7},{4,68},{5,1},{6,70},{7,3},{8,72},{9,13},... | collective-permute-start | bytes 208904 | tf_op jit(solution)/shard_map/ppermute | solution.py:421
  82.2 6.2 %collective-permute-start.24 = (f32[136,128]{1,0:T(8,128)S(1)}, f32[136,128]{1,0:T(8,128)S(1)}, u32[]{:S(2)}, u32[]{:S(2)}) collective-permute-start(f32[136,128]{1,0:T(8,128)S(1)} %add_add_fusion.mine), channel_id=1, source_target_pairs={{0,1},{1,0},{2,3},{3,2},{4,5},{5,4},{6,7},{7,6},{8,9},{9,8},{10,11... | collective-permute-start | bytes 208904 | tf_op jit(solution)/shard_map/ppermute | solution.py:386
  (1 other events, 2.8 us)

commit v2 on v1

--- a/solution.py
+++ b/solution.py
@@ -17,6 +17,7 @@
 HALF = RB * T
 VMEM_LIMIT = 16 << 20
 SKETCH_PIECES = 16
+CLOSE = 2e-3
 
 
 def split(a):
@@ -242,7 +243,9 @@
     )(s0, s1, vp, um, up, vm)
 
 
-def basis_kernel(root, mine, other, prod, basis, rfac, pack, a_ref, w_ref, e_ref):
+def basis_kernel(
+    root, mine, other, prod, basis, rfac, pack, a_ref, w_ref, e_ref, r_ref, out, out_sem, r_sem
+):
     core = lax.axis_index("col") & 1
 
     @pl.when(core == 0)
@@ -273,39 +276,45 @@
     dcol = lax.rsqrt(jnp.sum(masked, axis=1, keepdims=True))
     drow = lax.rsqrt(jnp.sum(masked, axis=0, keepdims=True))
     unit = jnp.where(eye, 0.0, a * dcol * drow)
-    e_ref[...] = unit
-    w_ref[...] = jnp.where(eye, 1.0, 0.0)
 
     def size(e):
-        return jnp.max(jnp.sum(jnp.abs(e), axis=0, keepdims=True))
+        return jnp.sum(jnp.sum(e * e, axis=0, keepdims=True))
+
+    def lower(e):
+        return jnp.where(rr > cc, e, jnp.where(eye, 0.5 * e, 0.0))
 
     def update(e):
-        phi = jnp.where(rr > cc, e, jnp.where(eye, 0.5 * e, 0.0)).astype(BF16)
+        phi = lower(e).astype(BF16)
         w = w_ref[...]
         t = dot(phi, w.astype(BF16))
-        w_ref[...] = w - t + dot(phi, t.astype(BF16))
+        return w - t + dot(phi, t.astype(BF16))
+
+    phi = lower(unit)
+    half = phi.astype(BF16)
+    w_ref[...] = jnp.where(eye, 1.0, 0.0) - phi + dot(half, half)
+
+    def residual():
+        w = w_ref[...]
+        t = dot3(w, jnp.where(eye, 1.0, unit))
+        e = dot3(t, w, ((1,), (1,))) - jnp.where(eye, 1.0, 0.0)
+        e_ref[...] = e
+        return size(e)
 
     def cond(state):
         it, err = state
-        return jnp.logical_and(err >= 0.01, it < 10)
+        return jnp.logical_and(err >= CLOSE, it < 10)
 
     def body(state):
         it, _ = state
-        update(e_ref[...])
-        w = w_ref[...]
-        scaled = jnp.where(eye, 1.0, unit)
-        t = dot3(w, scaled)
-        e = dot3(t, w, ((1,), (1,))) - jnp.where(eye, 1.0, 0.0)
-        e_ref[...] = e
-        return it + 1, size(e)
-
-    _, err = lax.while_loop(cond, body, (jnp.int32(0), size(unit)))
-    good = err < 0.01
+        w_ref[...] = update(e_ref[...])
+        return it + 1, residual()
+
+    _, err = lax.while_loop(cond, body, (jnp.int32(0), residual()))
+    good = err < CLOSE
 
     @pl.when(good)
     def _():
-        update(e_ref[...])
-        w_ref[...] = w_ref[...] * drow
+        w_ref[...] = update(e_ref[...]) * drow
 
     @pl.when(jnp.logical_not(good))
     def _():
@@ -330,14 +339,21 @@
         lax.fori_loop(0, K, step, 0)
 
     w = w_ref[...]
-    upper = dot3(w, a_ref[...])
-    rfac[...] = jnp.where(rr <= cc, upper, 0.0) * (1.0 / root)
     wh, wl = split(w * root)
+    dims = ((1,), (1,))
+    copies = []
     for j in range(4):
         rows = slice(j * 256, (j + 1) * 256)
         ph, plo = split(prod[rows, :])
-        dims = ((1,), (1,))
-        basis[rows, :] = dot(ph, wh, dims) + (dot(ph, wl, dims) + dot(plo, wh, dims))
+        out[rows, :] = dot(ph, wh, dims) + (dot(ph, wl, dims) + dot(plo, wh, dims))
+        copies.append(pltpu.make_async_copy(out.at[rows], basis.at[rows], out_sem.at[j]))
+        copies[-1].start()
+    upper = dot3(w, a_ref[...])
+    r_ref[...] = jnp.where(rr <= cc, upper, 0.0) * (1.0 / root)
+    copies.append(pltpu.make_async_copy(r_ref, rfac, r_sem))
+    copies[-1].start()
+    for copy in copies:
+        copy.wait()
 
 
 def finish(root, mine, other, prod):
@@ -345,8 +361,14 @@
     return pl.pallas_call(
         functools.partial(basis_kernel, root),
         in_specs=[vmem] * 3,
-        out_specs=[vmem] * 2,
-        scratch_shapes=[pltpu.VMEM((PACK, T), F32)] + [pltpu.VMEM((K, K), F32)] * 3,
+        out_specs=[pl.BlockSpec(memory_space=pltpu.HBM)] * 2,
+        scratch_shapes=[pltpu.VMEM((PACK, T), F32)]
+        + [pltpu.VMEM((K, K), F32)] * 4
+        + [
+            pltpu.VMEM((2 * HALF, K), F32),
+            pltpu.SemaphoreType.DMA((4,)),
+            pltpu.SemaphoreType.DMA,
+        ],
         out_shape=[
             jax.ShapeDtypeStruct((2 * HALF, K), F32),
             jax.ShapeDtypeStruct((K, K), F32),
@@ -399,8 +421,8 @@
         return spmm(items, at, meta, held, local, **kw)
 
     ca, cb = move(qa, partner), move(qb, partner)
-    d2p, d2m = sp(far_own, 0, held, adds=(ca, cb))
-    tp, tm = move(d2p, plus), move(d2m, minus)
+    fa, fb = sp(far_own, 0, held)
+    tp, tm = move(fa + ca, plus), move(fb + cb, minus)
     rest = u_other + v_other + u_own + here_other + v_own + here_own
     *qu, held = sp(u_other, 0, tiles, loads=rest)
     cu = [move(q, partner) for q in qu]
@@ -418,7 +440,7 @@
     tot = keep + move(send, partner)
     both = ("row", "col")
     for order in ORDERS:
-        got = [lax.ppermute(tot, both, axis_perm(order, by)) for by in (2, 3, 1)]
+        got = [lax.ppermute(tot, both, axis_perm(order, by)) for by in (3, 1, 2)]
         tot = (tot + got[0]) + (got[1] + got[2])
     rest = move(tot, partner)
     basis, rfac = finish(float(rows_all) ** 0.5, tot, rest, prod)

time: 132 us -> 128 us (0.970)
  waiting for transfers between devices: 38.4 us -> 32.9 us
  starting transfers between devices: 30.8 us -> 32.4 us
    ppermute x9, waiting for transfers between devices: 11.3 us -> 5.96 us  [on_device(): got = [lax.ppermute(tot, both, axis_perm(order, by)) for by in (3, 1, 2)]]
    ppermute x9, starting transfers between devices: 12.7 us -> 15.3 us  [on_device(): got = [lax.ppermute(tot, both, axis_perm(order, by)) for by in (3, 1, 2)]]
  transfers between devices with their start and end apart: 25 -> 25, of which waited for: 13 -> 10; matrix products, arithmetic and copies ran while one was open for 0% -> 0% of each run, Pallas kernels for 10% -> 11%
where the time goes in v2:
time: 128 us
  Pallas kernels  61.1 us (48%)
  waiting for transfers between devices  32.9 us (26%)
  starting transfers between devices  32.4 us (25%)
    pallas_call x1, Pallas kernels, finish(): pl.pallas_call(functools.partial(basis_kernel, root), in_specs=[vmem] * 3...  42.7 us
    ppermute x16, waiting for transfers between devices, move(): return lax.ppermute(q, 'col', to)  27 us
    ppermute x16, starting transfers between devices, move(): return lax.ppermute(q, 'col', to)  17.1 us
    ppermute x9, starting transfers between devices, on_device(): got = [lax.ppermute(tot, both, axis_perm(order, by)) for by in (3, 1, 2)]  15.3 us
    pallas_call x7, Pallas kernels, spmm(): pl.pallas_call(functools.partial(spmm_kernel, items, at, loads, len(adds)...  13.6 us
    ppermute x9, waiting for transfers between devices, on_device(): got = [lax.ppermute(tot, both, axis_perm(order, by)) for by in (3, 1, 2)]  5.96 us
    pallas_call x1, Pallas kernels, first(): pl.pallas_call(functools.partial(first_kernel, items, kept), in_specs=[hb...  4.13 us
  transfers between devices with their start and end apart: 25, of which 10 were waited for; matrix products, arithmetic and copies ran while one was open for 0% of the time, Pallas kernels for 11%

profile of v2, /device:TPU:1, one launch (start us, length us, event | category | flops | bytes accessed | tf_op | source)
XLA Modules:
  0.0 127.6 jit_solution(18304170315669712761)
XLA Ops:
  0.6 4.1 %first.1 = (f32[512,256]{1,0:T(8,128)S(1)}, f32[512,256]{1,0:T(8,128)S(1)}, bf16[8,8,128,128]{3,2,1,0:T(8,128)(2,1)S(1)}, bf16[8192,256]{1,0:T(8,128)(2,1)S(1)}) custom-call(s32[8,64]{1,0:T(8,128)} %bitcast.3, s32[1,64]{1,0:T(1,128)} %bitcast.19, f32[8,64]{1,0:T(8,128)} %bitcast.11, bf16[64,8,128,128]{3,2,1,0:T(8,128)(2,1)} %tiles.3, bf16[8192,256]{1,0:T(8,128)(2,1)} %sketch.1), custom_call_target="tpu_custom_call" | custom-call | flops 536870912 | bytes 8388608 | tf_op jit(solution)/shard_map/first/pallas_call | solution.py:118
  6.1 4.5 %spmm.7 = (f32[512,256]{1,0:T(8,128)S(1)}, f32[512,256]{1,0:T(8,128)S(1)}, bf16[48,8,128,128]{3,2,1,0:T(8,128)(2,1)S(1)}) custom-call(s32[8,64]{1,0:T(8,128)} %bitcast.4, s32[1,64]{1,0:T(1,128)} %bitcast.20, f32[8,64]{1,0:T(8,128)} %bitcast.12, bf16[64,8,128,128]{3,2,1,0:T(8,128)(2,1)} %tiles.3, bf16[8192,256]{1,0:T(8,128)(2,1)S(1)} %get-tuple-element.24.sketch), custom_call_target="tpu_custom_call" | custom-call | flops 536870912 | bytes 4194304 | tf_op jit(solution)/shard_map/spmm/pallas_call | solution.py:176
  13.2 1.5 %spmm.11 = (f32[512,256]{1,0:T(8,128)S(1)}, f32[512,256]{1,0:T(8,128)S(1)}) custom-call(s32[8,64]{1,0:T(8,128)} %bitcast.6, s32[1,64]{1,0:T(1,128)} %bitcast.22, f32[8,64]{1,0:T(8,128)} %bitcast.14, bf16[8,8,128,128]{3,2,1,0:T(8,128)(2,1)S(1)} %get-tuple-element.32.tiles, bf16[8192,256]{1,0:T(8,128)(2,1)S(1)} %get-tuple-element.24.sketch), custom_call_target="tpu_custom_call" | custom-call | flops 536870912 | bytes 4194304 | tf_op jit(solution)/shard_map/spmm/pallas_call | solution.py:176
  16.5 1.7 %collective-permute-start.7 = (f32[512,256]{1,0:T(8,128)S(1)}, f32[512,256]{1,0:T(8,128)S(1)}, u32[]{:S(2)}, u32[]{:S(2)}) collective-permute-start(f32[512,256]{1,0:T(8,128)S(1)} %add.37), channel_id=1, source_target_pairs={{0,6},{1,7},{2,0},{3,1},{4,2},{5,3},{6,4},{7,5},{8,14},{9,15},{10,... | collective-permute-start | bytes 1572872 | tf_op jit(solution)/shard_map/ppermute | solution.py:408
  18.2 1.5 %spmm.8 = (f32[512,256]{1,0:T(8,128)S(1)}, f32[512,256]{1,0:T(8,128)S(1)}) custom-call(s32[8,64]{1,0:T(8,128)} %bitcast.7, s32[1,64]{1,0:T(1,128)} %bitcast.23, f32[8,64]{1,0:T(8,128)} %bitcast.15, bf16[48,8,128,128]{3,2,1,0:T(8,128)(2,1)S(1)} %get-tuple-element.25.tiles, bf16[8192,256]{1,0:T(8,128)(2,1)S(1)} %get-tuple-element.24.sketch), custom_call_target="tpu_custom_call" | custom-call | flops 536870912 | bytes 4194304 | tf_op jit(solution)/shard_map/spmm/pallas_call | solution.py:176
  20.5 1.5 %spmm.13 = (f32[512,256]{1,0:T(8,128)S(1)}, f32[512,256]{1,0:T(8,128)S(1)}) custom-call(s32[8,64]{1,0:T(8,128)} %bitcast.8, s32[1,64]{1,0:T(1,128)} %bitcast.24, f32[8,64]{1,0:T(8,128)} %bitcast.16, bf16[48,8,128,128]{3,2,1,0:T(8,128)(2,1)S(1)} %get-tuple-element.25.tiles, bf16[8192,256]{1,0:T(8,128)(2,1)S(1)} %get-tuple-element.24.sketch, ...), custom_call_target="tpu_custom_call" | custom-call | flops 536870912 | bytes 4194304 | tf_op jit(solution)/shard_map/spmm/pallas_call | solution.py:176
  22.1 1.8 %collective-permute-start.11 = (f32[512,256]{1,0:T(8,128)S(1)}, f32[512,256]{1,0:T(8,128)S(1)}, u32[]{:S(2)}, u32[]{:S(2)}) collective-permute-start(f32[512,256]{1,0:T(8,128)S(1)} %get-tuple-element.40), channel_id=1, source_target_pairs={{0,6},{1,7},{2,0},{3,1},{4,2},{5,3},{6,4},{7,5},{8,14},{9,15},{10,... | collective-permute-start | bytes 1572872 | tf_op jit(solution)/shard_map/ppermute | solution.py:408
  23.9 6.1 %collective-permute-done.5.refs_2_ = f32[512,256]{1,0:T(8,128)S(1)} collective-permute-done((f32[512,256]{1,0:T(8,128)S(1)}, f32[512,256]{1,0:T(8,128)S(1)}, u32[]{:S(2)}, u32[]{:S(2)}) %collective-permute-start.5) | collective-permute-done | bytes 524320 | tf_op jit(solution)/shard_map/ppermute | solution.py:408
  30.0 1.5 %spmm.12 = (f32[512,256]{1,0:T(8,128)S(1)}, f32[512,256]{1,0:T(8,128)S(1)}) custom-call(s32[8,64]{1,0:T(8,128)} %bitcast.9, s32[1,64]{1,0:T(1,128)} %bitcast.25, f32[8,64]{1,0:T(8,128)} %bitcast.17, bf16[48,8,128,128]{3,2,1,0:T(8,128)(2,1)S(1)} %get-tuple-element.25.tiles, bf16[8192,256]{1,0:T(8,128)(2,1)S(1)} %get-tuple-element.24.sketch, ...), custom_call_target="tpu_custom_call" | custom-call | flops 536870912 | bytes 4194304 | tf_op jit(solution)/shard_map/spmm/pallas_call | solution.py:176
  32.7 1.6 %collective-permute-start.13 = (f32[512,256]{1,0:T(8,128)S(1)}, f32[512,256]{1,0:T(8,128)S(1)}, u32[]{:S(2)}, u32[]{:S(2)}) collective-permute-start(f32[512,256]{1,0:T(8,128)S(1)} %get-tuple-element.42), channel_id=1, source_target_pairs={{0,6},{1,7},{2,0},{3,1},{4,2},{5,3},{6,4},{7,5},{8,14},{9,15},{10,... | collective-permute-start | bytes 1572872 | tf_op jit(solution)/shard_map/ppermute | solution.py:408
  34.4 1.5 %spmm.9 = (f32[512,256]{1,0:T(8,128)S(1)}, f32[512,256]{1,0:T(8,128)S(1)}) custom-call(s32[8,64]{1,0:T(8,128)} %bitcast.10, s32[1,64]{1,0:T(1,128)} %bitcast.26, f32[8,64]{1,0:T(8,128)} %bitcast.18, bf16[48,8,128,128]{3,2,1,0:T(8,128)(2,1)S(1)} %get-tuple-element.25.tiles, bf16[8192,256]{1,0:T(8,128)(2,1)S(1)} %get-tuple-element.24.sketch, ...), custom_call_target="tpu_custom_call" | custom-call | flops 536870912 | bytes 4194304 | tf_op jit(solution)/shard_map/spmm/pallas_call | solution.py:176
  35.9 4.8 %collective-permute-done.11.um = f32[512,256]{1,0:T(8,128)S(1)} collective-permute-done((f32[512,256]{1,0:T(8,128)S(1)}, f32[512,256]{1,0:T(8,128)S(1)}, u32[]{:S(2)}, u32[]{:S(2)}) %collective-permute-start.11) | collective-permute-done | bytes 524320 | tf_op jit(solution)/shard_map/ppermute | solution.py:408
  40.7 3.0 %collective-permute-done.12.up = f32[512,256]{1,0:T(8,128)S(1)} collective-permute-done((f32[512,256]{1,0:T(8,128)S(1)}, f32[512,256]{1,0:T(8,128)S(1)}, u32[]{:S(2)}, u32[]{:S(2)}) %collective-permute-start.12) | collective-permute-done | bytes 524320 | tf_op jit(solution)/shard_map/ppermute | solution.py:408
  43.7 11.2 %collective-permute-done.8.vp = f32[512,256]{1,0:T(8,128)S(1)} collective-permute-done((f32[512,256]{1,0:T(8,128)S(1)}, f32[512,256]{1,0:T(8,128)S(1)}, u32[]{:S(2)}, u32[]{:S(2)}) %collective-permute-start.8) | collective-permute-done | bytes 524320 | tf_op jit(solution)/shard_map/ppermute | solution.py:408
  55.6 1.9 %collective-permute-start.14 = (f32[136,128]{1,0:T(8,128)S(1)}, f32[136,128]{1,0:T(8,128)S(1)}, u32[]{:S(2)}, u32[]{:S(2)}) collective-permute-start(f32[136,128]{1,0:T(8,128)S(1)} %get-tuple-element.44), channel_id=1, source_target_pairs={{0,1},{1,0},{2,3},{3,2},{4,5},{5,4},{6,7},{7,6},{8,9},{9,8},{10,11... | collective-permute-start | bytes 208904 | tf_op jit(solution)/shard_map/ppermute | solution.py:408
  58.4 3.0 %collective-permute-start.17 = (f32[136,128]{1,0:T(8,128)S(1)}, f32[136,128]{1,0:T(8,128)S(1)}, u32[]{:S(2)}, u32[]{:S(2)}) collective-permute-start(f32[136,128]{1,0:T(8,128)S(1)} %add.38), channel_id=1, source_target_pairs={{0,4},{1,17},{2,6},{3,19},{4,0},{5,21},{6,2},{7,23},{8,12},{9,25},... | collective-permute-start | bytes 208904 | tf_op jit(solution)/shard_map/ppermute | solution.py:443
  62.0 2.1 %collective-permute-start.15 = (f32[136,128]{1,0:T(8,128)S(1)}, f32[136,128]{1,0:T(8,128)S(1)}, u32[]{:S(2)}, u32[]{:S(2)}) collective-permute-start(f32[136,128]{1,0:T(8,128)S(1)} %add.38), channel_id=1, source_target_pairs={{0,6},{1,25},{2,0},{3,27},{4,2},{5,29},{6,4},{7,31},{8,14},{9,1},{... | collective-permute-start | bytes 208904 | tf_op jit(solution)/shard_map/ppermute | solution.py:443
  64.1 1.7 %collective-permute-done.16 = f32[136,128]{1,0:T(8,128)S(1)} collective-permute-done((f32[136,128]{1,0:T(8,128)S(1)}, f32[136,128]{1,0:T(8,128)S(1)}, u32[]{:S(2)}, u32[]{:S(2)}) %collective-permute-start.16) | collective-permute-done | bytes 69664 | tf_op jit(solution)/shard_map/ppermute | solution.py:443
  65.8 3.6 %collective-permute-start.20 = (f32[136,128]{1,0:T(8,128)S(1)}, f32[136,128]{1,0:T(8,128)S(1)}, u32[]{:S(2)}, u32[]{:S(2)}) collective-permute-start(f32[136,128]{1,0:T(8,128)S(1)} %add_add_fusion.2), channel_id=1, source_target_pairs={{0,16},{1,65},{2,18},{3,67},{4,20},{5,69},{6,22},{7,71},{8,24},{9,... | collective-permute-start | bytes 208904 | tf_op jit(solution)/shard_map/ppermute | solution.py:443
  70.2 1.9 %collective-permute-start.18 = (f32[136,128]{1,0:T(8,128)S(1)}, f32[136,128]{1,0:T(8,128)S(1)}, u32[]{:S(2)}, u32[]{:S(2)}) collective-permute-start(f32[136,128]{1,0:T(8,128)S(1)} %add_add_fusion.2), channel_id=1, source_target_pairs={{0,24},{1,97},{2,26},{3,99},{4,28},{5,101},{6,30},{7,103},{8,0},{9... | collective-permute-start | bytes 208904 | tf_op jit(solution)/shard_map/ppermute | solution.py:443
  72.1 1.8 %collective-permute-done.19 = f32[136,128]{1,0:T(8,128)S(1)} collective-permute-done((f32[136,128]{1,0:T(8,128)S(1)}, f32[136,128]{1,0:T(8,128)S(1)}, u32[]{:S(2)}, u32[]{:S(2)}) %collective-permute-start.19) | collective-permute-done | bytes 69664 | tf_op jit(solution)/shard_map/ppermute | solution.py:443
  74.5 2.7 %collective-permute-start.21 = (f32[136,128]{1,0:T(8,128)S(1)}, f32[136,128]{1,0:T(8,128)S(1)}, u32[]{:S(2)}, u32[]{:S(2)}) collective-permute-start(f32[136,128]{1,0:T(8,128)S(1)} %add_add_fusion.1), channel_id=1, source_target_pairs={{0,96},{1,7},{2,98},{3,1},{4,100},{5,3},{6,102},{7,5},{8,104},{9,1... | collective-permute-start | bytes 208904 | tf_op jit(solution)/shard_map/ppermute | solution.py:443
  79.7 4.1 %collective-permute-start.24 = (f32[136,128]{1,0:T(8,128)S(1)}, f32[136,128]{1,0:T(8,128)S(1)}, u32[]{:S(2)}, u32[]{:S(2)}) collective-permute-start(f32[136,128]{1,0:T(8,128)S(1)} %add_add_fusion.mine), channel_id=1, source_target_pairs={{0,1},{1,0},{2,3},{3,2},{4,5},{5,4},{6,7},{7,6},{8,9},{9,8},{10,11... | collective-permute-start | bytes 208904 | tf_op jit(solution)/shard_map/ppermute | solution.py:408
  84.7 42.7 %finish.1 = (f32[1024,256]{1,0:T(8,128)}, f32[256,256]{1,0:T(8,128)}) custom-call(f32[136,128]{1,0:T(8,128)S(1)} %add_add_fusion.mine, f32[136,128]{1,0:T(8,128)S(1)} %collective-permute-done.24.other, f32[1024,256]{1,0:T(8,128)S(1)} %get-tuple-element.45.prod), custom_call_target="tpu_custom_call" | custom-call | tf_op jit(solution)/shard_map/finish/pallas_call | solution.py:361
  (42 shorter events, 14.6 us)
Async XLA Ops:
  4.8 10.0 %collective-permute-start.4 = (f32[512,256]{1,0:T(8,128)S(1)}, f32[512,256]{1,0:T(8,128)S(1)}, u32[]{:S(2)}, u32[]{:S(2)}) collective-permute-start(f32[512,256]{1,0:T(8,128)S(1)} %get-tuple-element.34), channel_id=1, source_target_pairs={{0,1},{1,0},{2,3},{3,2},{4,5},{5,4},{6,7},{7,6},{8,9},{9,8},{10,11... | collective-permute-start | bytes 1572872 | tf_op jit(solution)/shard_map/ppermute | solution.py:408
  6.1 9.0 %collective-permute-start.6 = (f32[512,256]{1,0:T(8,128)S(1)}, f32[512,256]{1,0:T(8,128)S(1)}, u32[]{:S(2)}, u32[]{:S(2)}) collective-permute-start(f32[512,256]{1,0:T(8,128)S(1)} %get-tuple-element.36), channel_id=1, source_target_pairs={{0,1},{1,0},{2,3},{3,2},{4,5},{5,4},{6,7},{7,6},{8,9},{9,8},{10,11... | collective-permute-start | bytes 1572872 | tf_op jit(solution)/shard_map/ppermute | solution.py:408
  10.6 5.9 %collective-permute-start.9 = (f32[512,256]{1,0:T(8,128)S(1)}, f32[512,256]{1,0:T(8,128)S(1)}, u32[]{:S(2)}, u32[]{:S(2)}) collective-permute-start(f32[512,256]{1,0:T(8,128)S(1)} %get-tuple-element.38), channel_id=1, source_target_pairs={{0,1},{1,0},{2,3},{3,2},{4,5},{5,4},{6,7},{7,6},{8,9},{9,8},{10,11... | collective-permute-start | bytes 1572872 | tf_op jit(solution)/shard_map/ppermute | solution.py:408
  11.1 8.7 %collective-permute-start.10 = (f32[512,256]{1,0:T(8,128)S(1)}, f32[512,256]{1,0:T(8,128)S(1)}, u32[]{:S(2)}, u32[]{:S(2)}) collective-permute-start(f32[512,256]{1,0:T(8,128)S(1)} %get-tuple-element.39), channel_id=1, source_target_pairs={{0,1},{1,0},{2,3},{3,2},{4,5},{5,4},{6,7},{7,6},{8,9},{9,8},{10,11... | collective-permute-start | bytes 1572872 | tf_op jit(solution)/shard_map/ppermute | solution.py:408
  12.7 9.3 %collective-permute-start.2 = (f32[512,256]{1,0:T(8,128)S(1)}, f32[512,256]{1,0:T(8,128)S(1)}, u32[]{:S(2)}, u32[]{:S(2)}) collective-permute-start(f32[512,256]{1,0:T(8,128)S(1)} %get-tuple-element.30), channel_id=1, source_target_pairs={{0,1},{1,0},{2,3},{3,2},{4,5},{5,4},{6,7},{7,6},{8,9},{9,8},{10,11... | collective-permute-start | bytes 1572872 | tf_op jit(solution)/shard_map/ppermute | solution.py:408
  14.7 7.4 %collective-permute-start.3 = (f32[512,256]{1,0:T(8,128)S(1)}, f32[512,256]{1,0:T(8,128)S(1)}, u32[]{:S(2)}, u32[]{:S(2)}) collective-permute-start(f32[512,256]{1,0:T(8,128)S(1)} %get-tuple-element.31), channel_id=1, source_target_pairs={{0,1},{1,0},{2,3},{3,2},{4,5},{5,4},{6,7},{7,6},{8,9},{9,8},{10,11... | collective-permute-start | bytes 1572872 | tf_op jit(solution)/shard_map/ppermute | solution.py:408
  15.0 15.0 %collective-permute-start.5 = (f32[512,256]{1,0:T(8,128)S(1)}, f32[512,256]{1,0:T(8,128)S(1)}, u32[]{:S(2)}, u32[]{:S(2)}) collective-permute-start(f32[512,256]{1,0:T(8,128)S(1)} %add.36), channel_id=1, source_target_pairs={{0,2},{1,3},{2,4},{3,5},{4,6},{5,7},{6,0},{7,1},{8,10},{9,11},{10,... | collective-permute-start | bytes 1572872 | tf_op jit(solution)/shard_map/ppermute | solution.py:408
  16.5 13.5 %collective-permute-start.7 = (f32[512,256]{1,0:T(8,128)S(1)}, f32[512,256]{1,0:T(8,128)S(1)}, u32[]{:S(2)}, u32[]{:S(2)}) collective-permute-start(f32[512,256]{1,0:T(8,128)S(1)} %add.37), channel_id=1, source_target_pairs={{0,6},{1,7},{2,0},{3,1},{4,2},{5,3},{6,4},{7,5},{8,14},{9,15},{10,... | collective-permute-start | bytes 1572872 | tf_op jit(solution)/shard_map/ppermute | solution.py:408
  19.8 13.0 %collective-permute-start = (f32[512,256]{1,0:T(8,128)S(1)}, f32[512,256]{1,0:T(8,128)S(1)}, u32[]{:S(2)}, u32[]{:S(2)}) collective-permute-start(f32[512,256]{1,0:T(8,128)S(1)} %get-tuple-element.26), channel_id=1, source_target_pairs={{0,1},{1,0},{2,3},{3,2},{4,5},{5,4},{6,7},{7,6},{8,9},{9,8},{10,11... | collective-permute-start | bytes 1572872 | tf_op jit(solution)/shard_map/ppermute | solution.py:408
  22.0 12.4 %collective-permute-start.1 = (f32[512,256]{1,0:T(8,128)S(1)}, f32[512,256]{1,0:T(8,128)S(1)}, u32[]{:S(2)}, u32[]{:S(2)}) collective-permute-start(f32[512,256]{1,0:T(8,128)S(1)} %get-tuple-element.27), channel_id=1, source_target_pairs={{0,1},{1,0},{2,3},{3,2},{4,5},{5,4},{6,7},{7,6},{8,9},{9,8},{10,11... | collective-permute-start | bytes 1572872 | tf_op jit(solution)/shard_map/ppermute | solution.py:408
  22.1 18.6 %collective-permute-start.11 = (f32[512,256]{1,0:T(8,128)S(1)}, f32[512,256]{1,0:T(8,128)S(1)}, u32[]{:S(2)}, u32[]{:S(2)}) collective-permute-start(f32[512,256]{1,0:T(8,128)S(1)} %get-tuple-element.40), channel_id=1, source_target_pairs={{0,6},{1,7},{2,0},{3,1},{4,2},{5,3},{6,4},{7,5},{8,14},{9,15},{10,... | collective-permute-start | bytes 1572872 | tf_op jit(solution)/shard_map/ppermute | solution.py:408
  30.0 13.7 %collective-permute-start.12 = (f32[512,256]{1,0:T(8,128)S(1)}, f32[512,256]{1,0:T(8,128)S(1)}, u32[]{:S(2)}, u32[]{:S(2)}) collective-permute-start(f32[512,256]{1,0:T(8,128)S(1)} %get-tuple-element.41), channel_id=1, source_target_pairs={{0,2},{1,3},{2,4},{3,5},{4,6},{5,7},{6,0},{7,1},{8,10},{9,11},{10,... | collective-permute-start | bytes 1572872 | tf_op jit(solution)/shard_map/ppermute | solution.py:408
  31.5 23.4 %collective-permute-start.8 = (f32[512,256]{1,0:T(8,128)S(1)}, f32[512,256]{1,0:T(8,128)S(1)}, u32[]{:S(2)}, u32[]{:S(2)}) collective-permute-start(f32[512,256]{1,0:T(8,128)S(1)} %get-tuple-element.37), channel_id=1, source_target_pairs={{0,2},{1,3},{2,4},{3,5},{4,6},{5,7},{6,0},{7,1},{8,10},{9,11},{10,... | collective-permute-start | bytes 1572872 | tf_op jit(solution)/shard_map/ppermute | solution.py:408
  32.7 22.2 %collective-permute-start.13 = (f32[512,256]{1,0:T(8,128)S(1)}, f32[512,256]{1,0:T(8,128)S(1)}, u32[]{:S(2)}, u32[]{:S(2)}) collective-permute-start(f32[512,256]{1,0:T(8,128)S(1)} %get-tuple-element.42), channel_id=1, source_target_pairs={{0,6},{1,7},{2,0},{3,1},{4,2},{5,3},{6,4},{7,5},{8,14},{9,15},{10,... | collective-permute-start | bytes 1572872 | tf_op jit(solution)/shard_map/ppermute | solution.py:408
  58.4 5.7 %collective-permute-start.17 = (f32[136,128]{1,0:T(8,128)S(1)}, f32[136,128]{1,0:T(8,128)S(1)}, u32[]{:S(2)}, u32[]{:S(2)}) collective-permute-start(f32[136,128]{1,0:T(8,128)S(1)} %add.38), channel_id=1, source_target_pairs={{0,4},{1,17},{2,6},{3,19},{4,0},{5,21},{6,2},{7,23},{8,12},{9,25},... | collective-permute-start | bytes 208904 | tf_op jit(solution)/shard_map/ppermute | solution.py:443
  61.4 4.4 %collective-permute-start.16 = (f32[136,128]{1,0:T(8,128)S(1)}, f32[136,128]{1,0:T(8,128)S(1)}, u32[]{:S(2)}, u32[]{:S(2)}) collective-permute-start(f32[136,128]{1,0:T(8,128)S(1)} %add.38), channel_id=1, source_target_pairs={{0,2},{1,9},{2,4},{3,11},{4,6},{5,13},{6,0},{7,15},{8,10},{9,17},{... | collective-permute-start | bytes 208904 | tf_op jit(solution)/shard_map/ppermute | solution.py:443
  62.0 3.8 %collective-permute-start.15 = (f32[136,128]{1,0:T(8,128)S(1)}, f32[136,128]{1,0:T(8,128)S(1)}, u32[]{:S(2)}, u32[]{:S(2)}) collective-permute-start(f32[136,128]{1,0:T(8,128)S(1)} %add.38), channel_id=1, source_target_pairs={{0,6},{1,25},{2,0},{3,27},{4,2},{5,29},{6,4},{7,31},{8,14},{9,1},{... | collective-permute-start | bytes 208904 | tf_op jit(solution)/shard_map/ppermute | solution.py:443
  65.8 6.3 %collective-permute-start.20 = (f32[136,128]{1,0:T(8,128)S(1)}, f32[136,128]{1,0:T(8,128)S(1)}, u32[]{:S(2)}, u32[]{:S(2)}) collective-permute-start(f32[136,128]{1,0:T(8,128)S(1)} %add_add_fusion.2), channel_id=1, source_target_pairs={{0,16},{1,65},{2,18},{3,67},{4,20},{5,69},{6,22},{7,71},{8,24},{9,... | collective-permute-start | bytes 208904 | tf_op jit(solution)/shard_map/ppermute | solution.py:443
  69.4 4.4 %collective-permute-start.19 = (f32[136,128]{1,0:T(8,128)S(1)}, f32[136,128]{1,0:T(8,128)S(1)}, u32[]{:S(2)}, u32[]{:S(2)}) collective-permute-start(f32[136,128]{1,0:T(8,128)S(1)} %add_add_fusion.2), channel_id=1, source_target_pairs={{0,8},{1,33},{2,10},{3,35},{4,12},{5,37},{6,14},{7,39},{8,16},{9,4... | collective-permute-start | bytes 208904 | tf_op jit(solution)/shard_map/ppermute | solution.py:443
  70.2 3.6 %collective-permute-start.18 = (f32[136,128]{1,0:T(8,128)S(1)}, f32[136,128]{1,0:T(8,128)S(1)}, u32[]{:S(2)}, u32[]{:S(2)}) collective-permute-start(f32[136,128]{1,0:T(8,128)S(1)} %add_add_fusion.2), channel_id=1, source_target_pairs={{0,24},{1,97},{2,26},{3,99},{4,28},{5,101},{6,30},{7,103},{8,0},{9... | collective-permute-start | bytes 208904 | tf_op jit(solution)/shard_map/ppermute | solution.py:443
  73.9 4.8 %collective-permute-start.23 = (f32[136,128]{1,0:T(8,128)S(1)}, f32[136,128]{1,0:T(8,128)S(1)}, u32[]{:S(2)}, u32[]{:S(2)}) collective-permute-start(f32[136,128]{1,0:T(8,128)S(1)} %add_add_fusion.1), channel_id=1, source_target_pairs={{0,64},{1,5},{2,66},{3,7},{4,68},{5,1},{6,70},{7,3},{8,72},{9,13},... | collective-permute-start | bytes 208904 | tf_op jit(solution)/shard_map/ppermute | solution.py:443
  74.5 5.2 %collective-permute-start.22 = (f32[136,128]{1,0:T(8,128)S(1)}, f32[136,128]{1,0:T(8,128)S(1)}, u32[]{:S(2)}, u32[]{:S(2)}) collective-permute-start(f32[136,128]{1,0:T(8,128)S(1)} %add_add_fusion.1), channel_id=1, source_target_pairs={{0,32},{1,3},{2,34},{3,5},{4,36},{5,7},{6,38},{7,1},{8,40},{9,11},... | collective-permute-start | bytes 208904 | tf_op jit(solution)/shard_map/ppermute | solution.py:443
  74.5 5.2 %collective-permute-start.21 = (f32[136,128]{1,0:T(8,128)S(1)}, f32[136,128]{1,0:T(8,128)S(1)}, u32[]{:S(2)}, u32[]{:S(2)}) collective-permute-start(f32[136,128]{1,0:T(8,128)S(1)} %add_add_fusion.1), channel_id=1, source_target_pairs={{0,96},{1,7},{2,98},{3,1},{4,100},{5,3},{6,102},{7,5},{8,104},{9,1... | collective-permute-start | bytes 208904 | tf_op jit(solution)/shard_map/ppermute | solution.py:443
  79.7 5.0 %collective-permute-start.24 = (f32[136,128]{1,0:T(8,128)S(1)}, f32[136,128]{1,0:T(8,128)S(1)}, u32[]{:S(2)}, u32[]{:S(2)}) collective-permute-start(f32[136,128]{1,0:T(8,128)S(1)} %add_add_fusion.mine), channel_id=1, source_target_pairs={{0,1},{1,0},{2,3},{3,2},{4,5},{5,4},{6,7},{7,6},{8,9},{9,8},{10,11... | collective-permute-start | bytes 208904 | tf_op jit(solution)/shard_map/ppermute | solution.py:408
  (1 other events, 2.8 us)

commit v3 on v2

--- a/solution.py
+++ b/solution.py
@@ -16,8 +16,8 @@
 K = 256
 HALF = RB * T
 VMEM_LIMIT = 16 << 20
-SKETCH_PIECES = 16
-CLOSE = 2e-3
+SKETCH_PIECES = 4
+CLOSE = 4e-3
 
 
 def split(a):
@@ -30,9 +30,10 @@
 
 
 def dot3(a, b, dims=((1,), (0,))):
-    ah, al = split(a)
-    bh, bl = split(b)
-    return dot(ah, bh, dims) + (dot(ah, bl, dims) + dot(al, bh, dims))
+    ah, al = a if isinstance(a, tuple) else split(a)
+    bh, bl = b if isinstance(b, tuple) else split(b)
+    (ca,), (cb,) = dims
+    return dot(jnp.concatenate([ah, ah, al], ca), jnp.concatenate([bh, bl, bh], cb), dims)
 
 
 def first_row(me, item):
@@ -201,15 +202,13 @@
         p = (s0, s1)[h][rows, :] + (first[rows, :] + second[rows, :])
         prod[j * chunk:(j + 1) * chunk, :] = p
         hi, lo = split(p)
-        main = dot(hi, hi, ((0,), (0,)))
-        cross = dot(hi, lo, ((0,), (0,)))
+        both = dot(hi, jnp.concatenate([hi, lo], axis=1), ((0,), (0,)))
         if j == 0:
-            acc[0] = main
-            acc[1] = cross
+            acc[...] = both
         else:
-            acc[0] += main
-            acc[1] += cross
-    g = acc[0] + (acc[1] + acc[1].T)
+            acc[...] += both
+    cross = acc[:, K:]
+    g = acc[:, :K] + (cross + cross.T)
     low = g[T:, T:]
     r = lax.broadcasted_iota(jnp.int32, (T, T), 0)
     c = lax.broadcasted_iota(jnp.int32, (T, T), 1)
@@ -235,7 +234,7 @@
         gram_kernel,
         in_specs=[vmem] * 6,
         out_specs=[vmem] * 3,
-        scratch_shapes=[pltpu.VMEM((2, K, K), F32), pltpu.VMEM((PACK, T), F32)],
+        scratch_shapes=[pltpu.VMEM((K, 2 * K), F32), pltpu.VMEM((PACK, T), F32)],
         out_shape=[jax.ShapeDtypeStruct((2 * HALF, K), F32)]
         + [jax.ShapeDtypeStruct((PH, T), F32)] * 2,
         compiler_params=pltpu.CompilerParams(vmem_limit_bytes=VMEM_LIMIT),
@@ -283,15 +282,16 @@
     def lower(e):
         return jnp.where(rr > cc, e, jnp.where(eye, 0.5 * e, 0.0))
 
+    def change(e):
+        p = lower(e)
+        h = p.astype(BF16)
+        return dot(h, h) + lower(dot(h, h, ((1,), (1,)))) - p
+
     def update(e):
-        phi = lower(e).astype(BF16)
         w = w_ref[...]
-        t = dot(phi, w.astype(BF16))
-        return w - t + dot(phi, t.astype(BF16))
-
-    phi = lower(unit)
-    half = phi.astype(BF16)
-    w_ref[...] = jnp.where(eye, 1.0, 0.0) - phi + dot(half, half)
+        return w + dot(change(e).astype(BF16), w.astype(BF16))
+
+    w_ref[...] = jnp.where(eye, 1.0, 0.0) + change(unit)
 
     def residual():
         w = w_ref[...]
@@ -339,13 +339,11 @@
         lax.fori_loop(0, K, step, 0)
 
     w = w_ref[...]
-    wh, wl = split(w * root)
-    dims = ((1,), (1,))
+    scaled = split(w * root)
     copies = []
     for j in range(4):
         rows = slice(j * 256, (j + 1) * 256)
-        ph, plo = split(prod[rows, :])
-        out[rows, :] = dot(ph, wh, dims) + (dot(ph, wl, dims) + dot(plo, wh, dims))
+        out[rows, :] = dot3(prod[rows, :], scaled, ((1,), (1,)))
         copies.append(pltpu.make_async_copy(out.at[rows], basis.at[rows], out_sem.at[j]))
         copies[-1].start()
     upper = dot3(w, a_ref[...])
@@ -378,7 +376,7 @@
     )(mine, other, prod)
 
 
-ORDERS = ((2, 1), (1, 0), (0, 2))
+ORDERS = ((0, 1), (1, 2), (2, 0))
 
 
 def perm(size, target):
@@ -423,18 +421,17 @@
     ca, cb = move(qa, partner), move(qb, partner)
     fa, fb = sp(far_own, 0, held)
     tp, tm = move(fa + ca, plus), move(fb + cb, minus)
-    rest = u_other + v_other + u_own + here_other + v_own + here_own
-    *qu, held = sp(u_other, 0, tiles, loads=rest)
+    *qu, held = sp(u_other, 0, tiles, loads=u_other + u_own)
     cu = [move(q, partner) for q in qu]
-    qv = sp(v_other, 2, held)
+    fu = sp(u_own, 2, held)
+    up, um = move(fu[0] + cu[0], plus), move(fu[1] + cu[1], minus)
+    *qv, held = sp(v_other, 0, tiles, loads=v_other + v_own + here_other + here_own)
     cv = [move(q, partner) for q in qv]
-    up, um = sp(u_own, 4, held, adds=cu)
-    up, um = move(up, plus), move(um, minus)
-    qo = sp(here_other, 6, held)
+    qo = sp(here_other, 4, held)
     co = [move(q, partner) for q in qo]
-    vp, vm = sp(v_own, 8, held, adds=(*cv, tp, tm))
+    vp, vm = sp(v_own, 2, held, adds=(*cv, tp, tm))
     vp, vm = move(vp, plus), move(vm, minus)
-    s0, s1 = sp(here_own, 10, held, adds=co)
+    s0, s1 = sp(here_own, 6, held, adds=co)
 
     prod, keep, send = gram(s0, s1, vp, um, up, vm)
     tot = keep + move(send, partner)

time: 128 us -> 128 us (level)
  no operation moved by 1% of the time
where the time goes in v3:
time: 128 us
  Pallas kernels  61.5 us (48%)
  starting transfers between devices  33.2 us (26%)
  waiting for transfers between devices  32.1 us (25%)
    pallas_call x1, Pallas kernels, finish(): pl.pallas_call(functools.partial(basis_kernel, root), in_specs=[vmem] * 3...  42.7 us
    ppermute x16, waiting for transfers between devices, move(): return lax.ppermute(q, 'col', to)  26.6 us
    ppermute x16, starting transfers between devices, move(): return lax.ppermute(q, 'col', to)  17.6 us
    ppermute x9, starting transfers between devices, on_device(): got = [lax.ppermute(tot, both, axis_perm(order, by)) for by in (3, 1, 2)]  15.6 us
    pallas_call x7, Pallas kernels, spmm(): pl.pallas_call(functools.partial(spmm_kernel, items, at, loads, len(adds)...  14.2 us
    ppermute x9, waiting for transfers between devices, on_device(): got = [lax.ppermute(tot, both, axis_perm(order, by)) for by in (3, 1, 2)]  5.46 us
    pallas_call x1, Pallas kernels, first(): pl.pallas_call(functools.partial(first_kernel, items, kept), in_specs=[hb...  4.03 us
  transfers between devices with their start and end apart: 25, of which 10 were waited for; matrix products, arithmetic and copies ran while one was open for 0% of the time, Pallas kernels for 11%

profile of v3, /device:TPU:1, one launch (start us, length us, event | category | flops | bytes accessed | tf_op | source)
XLA Modules:
  0.0 128.0 jit_solution(10947290483949111554)
XLA Ops:
  0.6 4.0 %first.1 = (f32[512,256]{1,0:T(8,128)S(1)}, f32[512,256]{1,0:T(8,128)S(1)}, bf16[8,8,128,128]{3,2,1,0:T(8,128)(2,1)S(1)}, bf16[8192,256]{1,0:T(8,128)(2,1)S(1)}) custom-call(s32[8,64]{1,0:T(8,128)} %bitcast.3, s32[1,64]{1,0:T(1,128)} %bitcast.19, f32[8,64]{1,0:T(8,128)} %bitcast.11, bf16[64,8,128,128]{3,2,1,0:T(8,128)(2,1)} %tiles.5, bf16[8192,256]{1,0:T(8,128)(2,1)} %sketch.1), custom_call_target="tpu_custom_call" | custom-call | flops 536870912 | bytes 8388608 | tf_op jit(solution)/shard_map/first/pallas_call | solution.py:119
  6.0 3.1 %spmm.12 = (f32[512,256]{1,0:T(8,128)S(1)}, f32[512,256]{1,0:T(8,128)S(1)}, bf16[16,8,128,128]{3,2,1,0:T(8,128)(2,1)S(1)}) custom-call(s32[8,64]{1,0:T(8,128)} %bitcast.4, s32[1,64]{1,0:T(1,128)} %bitcast.20, f32[8,64]{1,0:T(8,128)} %bitcast.12, bf16[64,8,128,128]{3,2,1,0:T(8,128)(2,1)} %tiles.5, bf16[8192,256]{1,0:T(8,128)(2,1)S(1)} %get-tuple-element.25.sketch), custom_call_target="tpu_custom_call" | custom-call | flops 536870912 | bytes 4194304 | tf_op jit(solution)/shard_map/spmm/pallas_call | solution.py:177
  9.7 3.5 %spmm.7 = (f32[512,256]{1,0:T(8,128)S(1)}, f32[512,256]{1,0:T(8,128)S(1)}, bf16[32,8,128,128]{3,2,1,0:T(8,128)(2,1)S(1)}) custom-call(s32[8,64]{1,0:T(8,128)} %bitcast.5, s32[1,64]{1,0:T(1,128)} %bitcast.21, f32[8,64]{1,0:T(8,128)} %bitcast.13, bf16[64,8,128,128]{3,2,1,0:T(8,128)(2,1)} %tiles.5, bf16[8192,256]{1,0:T(8,128)(2,1)S(1)} %get-tuple-element.25.sketch), custom_call_target="tpu_custom_call" | custom-call | flops 536870912 | bytes 4194304 | tf_op jit(solution)/shard_map/spmm/pallas_call | solution.py:177
  13.8 1.5 %spmm.10 = (f32[512,256]{1,0:T(8,128)S(1)}, f32[512,256]{1,0:T(8,128)S(1)}) custom-call(s32[8,64]{1,0:T(8,128)} %bitcast.6, s32[1,64]{1,0:T(1,128)} %bitcast.22, f32[8,64]{1,0:T(8,128)} %bitcast.14, bf16[8,8,128,128]{3,2,1,0:T(8,128)(2,1)S(1)} %get-tuple-element.33.tiles, bf16[8192,256]{1,0:T(8,128)(2,1)S(1)} %get-tuple-element.25.sketch), custom_call_target="tpu_custom_call" | custom-call | flops 536870912 | bytes 4194304 | tf_op jit(solution)/shard_map/spmm/pallas_call | solution.py:177
  17.0 1.7 %collective-permute-start.7 = (f32[512,256]{1,0:T(8,128)S(1)}, f32[512,256]{1,0:T(8,128)S(1)}, u32[]{:S(2)}, u32[]{:S(2)}) collective-permute-start(f32[512,256]{1,0:T(8,128)S(1)} %add.43), channel_id=1, source_target_pairs={{0,6},{1,7},{2,0},{3,1},{4,2},{5,3},{6,4},{7,5},{8,14},{9,15},{10,... | collective-permute-start | bytes 1572872 | tf_op jit(solution)/shard_map/ppermute | solution.py:406
  21.0 1.5 %spmm.13 = (f32[512,256]{1,0:T(8,128)S(1)}, f32[512,256]{1,0:T(8,128)S(1)}) custom-call(s32[8,64]{1,0:T(8,128)} %bitcast.8, s32[1,64]{1,0:T(1,128)} %bitcast.24, f32[8,64]{1,0:T(8,128)} %bitcast.16, bf16[16,8,128,128]{3,2,1,0:T(8,128)(2,1)S(1)} %get-tuple-element.39.tiles, bf16[8192,256]{1,0:T(8,128)(2,1)S(1)} %get-tuple-element.25.sketch), custom_call_target="tpu_custom_call" | custom-call | flops 536870912 | bytes 4194304 | tf_op jit(solution)/shard_map/spmm/pallas_call | solution.py:177
  22.9 1.7 %collective-permute-start.10 = (f32[512,256]{1,0:T(8,128)S(1)}, f32[512,256]{1,0:T(8,128)S(1)}, u32[]{:S(2)}, u32[]{:S(2)}) collective-permute-start(f32[512,256]{1,0:T(8,128)S(1)} %add.44), channel_id=1, source_target_pairs={{0,6},{1,7},{2,0},{3,1},{4,2},{5,3},{6,4},{7,5},{8,14},{9,15},{10,... | collective-permute-start | bytes 1572872 | tf_op jit(solution)/shard_map/ppermute | solution.py:406
  24.6 5.8 %collective-permute-done.5.refs_2_ = f32[512,256]{1,0:T(8,128)S(1)} collective-permute-done((f32[512,256]{1,0:T(8,128)S(1)}, f32[512,256]{1,0:T(8,128)S(1)}, u32[]{:S(2)}, u32[]{:S(2)}) %collective-permute-start.5) | collective-permute-done | bytes 524320 | tf_op jit(solution)/shard_map/ppermute | solution.py:406
  30.4 1.5 %spmm.11 = (f32[512,256]{1,0:T(8,128)S(1)}, f32[512,256]{1,0:T(8,128)S(1)}) custom-call(s32[8,64]{1,0:T(8,128)} %bitcast.9, s32[1,64]{1,0:T(1,128)} %bitcast.25, f32[8,64]{1,0:T(8,128)} %bitcast.17, bf16[32,8,128,128]{3,2,1,0:T(8,128)(2,1)S(1)} %get-tuple-element.26.tiles, bf16[8192,256]{1,0:T(8,128)(2,1)S(1)} %get-tuple-element.25.sketch, ...), custom_call_target="tpu_custom_call" | custom-call | flops 536870912 | bytes 4194304 | tf_op jit(solution)/shard_map/spmm/pallas_call | solution.py:177
  31.9 1.6 %collective-permute-start.8 = (f32[512,256]{1,0:T(8,128)S(1)}, f32[512,256]{1,0:T(8,128)S(1)}, u32[]{:S(2)}, u32[]{:S(2)}) collective-permute-start(f32[512,256]{1,0:T(8,128)S(1)} %get-tuple-element.38), channel_id=1, source_target_pairs={{0,2},{1,3},{2,4},{3,5},{4,6},{5,7},{6,0},{7,1},{8,10},{9,11},{10,... | collective-permute-start | bytes 1572872 | tf_op jit(solution)/shard_map/ppermute | solution.py:406
  34.8 1.5 %spmm.9 = (f32[512,256]{1,0:T(8,128)S(1)}, f32[512,256]{1,0:T(8,128)S(1)}) custom-call(s32[8,64]{1,0:T(8,128)} %bitcast.10, s32[1,64]{1,0:T(1,128)} %bitcast.26, f32[8,64]{1,0:T(8,128)} %bitcast.18, bf16[32,8,128,128]{3,2,1,0:T(8,128)(2,1)S(1)} %get-tuple-element.26.tiles, bf16[8192,256]{1,0:T(8,128)(2,1)S(1)} %get-tuple-element.25.sketch, ...), custom_call_target="tpu_custom_call" | custom-call | flops 536870912 | bytes 4194304 | tf_op jit(solution)/shard_map/spmm/pallas_call | solution.py:177
  36.3 5.2 %collective-permute-done.10.um = f32[512,256]{1,0:T(8,128)S(1)} collective-permute-done((f32[512,256]{1,0:T(8,128)S(1)}, f32[512,256]{1,0:T(8,128)S(1)}, u32[]{:S(2)}, u32[]{:S(2)}) %collective-permute-start.10) | collective-permute-done | bytes 524320 | tf_op jit(solution)/shard_map/ppermute | solution.py:406
  41.5 2.5 %collective-permute-done.12.up = f32[512,256]{1,0:T(8,128)S(1)} collective-permute-done((f32[512,256]{1,0:T(8,128)S(1)}, f32[512,256]{1,0:T(8,128)S(1)}, u32[]{:S(2)}, u32[]{:S(2)}) %collective-permute-start.12) | collective-permute-done | bytes 524320 | tf_op jit(solution)/shard_map/ppermute | solution.py:406
  44.0 11.2 %collective-permute-done.8.vp = f32[512,256]{1,0:T(8,128)S(1)} collective-permute-done((f32[512,256]{1,0:T(8,128)S(1)}, f32[512,256]{1,0:T(8,128)S(1)}, u32[]{:S(2)}, u32[]{:S(2)}) %collective-permute-start.8) | collective-permute-done | bytes 524320 | tf_op jit(solution)/shard_map/ppermute | solution.py:406
  55.9 2.0 %collective-permute-start.14 = (f32[136,128]{1,0:T(8,128)S(1)}, f32[136,128]{1,0:T(8,128)S(1)}, u32[]{:S(2)}, u32[]{:S(2)}) collective-permute-start(f32[136,128]{1,0:T(8,128)S(1)} %get-tuple-element.46), channel_id=1, source_target_pairs={{0,1},{1,0},{2,3},{3,2},{4,5},{5,4},{6,7},{7,6},{8,9},{9,8},{10,11... | collective-permute-start | bytes 208904 | tf_op jit(solution)/shard_map/ppermute | solution.py:406
  58.8 3.4 %collective-permute-start.17 = (f32[136,128]{1,0:T(8,128)S(1)}, f32[136,128]{1,0:T(8,128)S(1)}, u32[]{:S(2)}, u32[]{:S(2)}) collective-permute-start(f32[136,128]{1,0:T(8,128)S(1)} %add.46), channel_id=1, source_target_pairs={{0,64},{1,17},{2,66},{3,19},{4,68},{5,21},{6,70},{7,23},{8,72},{9,... | collective-permute-start | bytes 208904 | tf_op jit(solution)/shard_map/ppermute | solution.py:440
  62.3 2.5 %collective-permute-start.15 = (f32[136,128]{1,0:T(8,128)S(1)}, f32[136,128]{1,0:T(8,128)S(1)}, u32[]{:S(2)}, u32[]{:S(2)}) collective-permute-start(f32[136,128]{1,0:T(8,128)S(1)} %add.46), channel_id=1, source_target_pairs={{0,96},{1,25},{2,98},{3,27},{4,100},{5,29},{6,102},{7,31},{8,104},... | collective-permute-start | bytes 208904 | tf_op jit(solution)/shard_map/ppermute | solution.py:440
  64.8 1.7 %collective-permute-done.16 = f32[136,128]{1,0:T(8,128)S(1)} collective-permute-done((f32[136,128]{1,0:T(8,128)S(1)}, f32[136,128]{1,0:T(8,128)S(1)}, u32[]{:S(2)}, u32[]{:S(2)}) %collective-permute-start.16) | collective-permute-done | bytes 69664 | tf_op jit(solution)/shard_map/ppermute | solution.py:440
  67.3 2.7 %collective-permute-start.18 = (f32[136,128]{1,0:T(8,128)S(1)}, f32[136,128]{1,0:T(8,128)S(1)}, u32[]{:S(2)}, u32[]{:S(2)}) collective-permute-start(f32[136,128]{1,0:T(8,128)S(1)} %add_add_fusion.2), channel_id=1, source_target_pairs={{0,24},{1,7},{2,26},{3,1},{4,28},{5,3},{6,30},{7,5},{8,0},{9,15},{... | collective-permute-start | bytes 208904 | tf_op jit(solution)/shard_map/ppermute | solution.py:440
  72.1 3.4 %collective-permute-start.23 = (f32[136,128]{1,0:T(8,128)S(1)}, f32[136,128]{1,0:T(8,128)S(1)}, u32[]{:S(2)}, u32[]{:S(2)}) collective-permute-start(f32[136,128]{1,0:T(8,128)S(1)} %add_add_fusion.1), channel_id=1, source_target_pairs={{0,4},{1,65},{2,6},{3,67},{4,0},{5,69},{6,2},{7,71},{8,12},{9,73},... | collective-permute-start | bytes 208904 | tf_op jit(solution)/shard_map/ppermute | solution.py:440
  76.2 2.0 %collective-permute-start.21 = (f32[136,128]{1,0:T(8,128)S(1)}, f32[136,128]{1,0:T(8,128)S(1)}, u32[]{:S(2)}, u32[]{:S(2)}) collective-permute-start(f32[136,128]{1,0:T(8,128)S(1)} %add_add_fusion.1), channel_id=1, source_target_pairs={{0,6},{1,97},{2,0},{3,99},{4,2},{5,101},{6,4},{7,103},{8,14},{9,10... | collective-permute-start | bytes 208904 | tf_op jit(solution)/shard_map/ppermute | solution.py:440
  78.1 1.7 %collective-permute-done.22 = f32[136,128]{1,0:T(8,128)S(1)} collective-permute-done((f32[136,128]{1,0:T(8,128)S(1)}, f32[136,128]{1,0:T(8,128)S(1)}, u32[]{:S(2)}, u32[]{:S(2)}) %collective-permute-start.22) | collective-permute-done | bytes 69664 | tf_op jit(solution)/shard_map/ppermute | solution.py:440
  79.9 4.4 %collective-permute-start.24 = (f32[136,128]{1,0:T(8,128)S(1)}, f32[136,128]{1,0:T(8,128)S(1)}, u32[]{:S(2)}, u32[]{:S(2)}) collective-permute-start(f32[136,128]{1,0:T(8,128)S(1)} %add_add_fusion.mine), channel_id=1, source_target_pairs={{0,1},{1,0},{2,3},{3,2},{4,5},{5,4},{6,7},{7,6},{8,9},{9,8},{10,11... | collective-permute-start | bytes 208904 | tf_op jit(solution)/shard_map/ppermute | solution.py:406
  85.2 42.7 %finish.1 = (f32[1024,256]{1,0:T(8,128)}, f32[256,256]{1,0:T(8,128)}) custom-call(f32[136,128]{1,0:T(8,128)S(1)} %add_add_fusion.mine, f32[136,128]{1,0:T(8,128)S(1)} %collective-permute-done.24.other, f32[1024,256]{1,0:T(8,128)S(1)} %get-tuple-element.47.prod), custom_call_target="tpu_custom_call" | custom-call | tf_op jit(solution)/shard_map/finish/pallas_call | solution.py:359
  (44 shorter events, 14.2 us)
Async XLA Ops:
  4.7 10.6 %collective-permute-start.4 = (f32[512,256]{1,0:T(8,128)S(1)}, f32[512,256]{1,0:T(8,128)S(1)}, u32[]{:S(2)}, u32[]{:S(2)}) collective-permute-start(f32[512,256]{1,0:T(8,128)S(1)} %get-tuple-element.35), channel_id=1, source_target_pairs={{0,1},{1,0},{2,3},{3,2},{4,5},{5,4},{6,7},{7,6},{8,9},{9,8},{10,11... | collective-permute-start | bytes 1572872 | tf_op jit(solution)/shard_map/ppermute | solution.py:406
  5.9 9.6 %collective-permute-start.6 = (f32[512,256]{1,0:T(8,128)S(1)}, f32[512,256]{1,0:T(8,128)S(1)}, u32[]{:S(2)}, u32[]{:S(2)}) collective-permute-start(f32[512,256]{1,0:T(8,128)S(1)} %get-tuple-element.37), channel_id=1, source_target_pairs={{0,1},{1,0},{2,3},{3,2},{4,5},{5,4},{6,7},{7,6},{8,9},{9,8},{10,11... | collective-permute-start | bytes 1572872 | tf_op jit(solution)/shard_map/ppermute | solution.py:406
  9.1 7.9 %collective-permute-start.9 = (f32[512,256]{1,0:T(8,128)S(1)}, f32[512,256]{1,0:T(8,128)S(1)}, u32[]{:S(2)}, u32[]{:S(2)}) collective-permute-start(f32[512,256]{1,0:T(8,128)S(1)} %get-tuple-element.41), channel_id=1, source_target_pairs={{0,1},{1,0},{2,3},{3,2},{4,5},{5,4},{6,7},{7,6},{8,9},{9,8},{10,11... | collective-permute-start | bytes 1572872 | tf_op jit(solution)/shard_map/ppermute | solution.py:406
  9.6 10.6 %collective-permute-start.11 = (f32[512,256]{1,0:T(8,128)S(1)}, f32[512,256]{1,0:T(8,128)S(1)}, u32[]{:S(2)}, u32[]{:S(2)}) collective-permute-start(f32[512,256]{1,0:T(8,128)S(1)} %get-tuple-element.43), channel_id=1, source_target_pairs={{0,1},{1,0},{2,3},{3,2},{4,5},{5,4},{6,7},{7,6},{8,9},{9,8},{10,11... | collective-permute-start | bytes 1572872 | tf_op jit(solution)/shard_map/ppermute | solution.py:406
  13.3 9.5 %collective-permute-start.2 = (f32[512,256]{1,0:T(8,128)S(1)}, f32[512,256]{1,0:T(8,128)S(1)}, u32[]{:S(2)}, u32[]{:S(2)}) collective-permute-start(f32[512,256]{1,0:T(8,128)S(1)} %get-tuple-element.31), channel_id=1, source_target_pairs={{0,1},{1,0},{2,3},{3,2},{4,5},{5,4},{6,7},{7,6},{8,9},{9,8},{10,11... | collective-permute-start | bytes 1572872 | tf_op jit(solution)/shard_map/ppermute | solution.py:406
  15.3 7.5 %collective-permute-start.3 = (f32[512,256]{1,0:T(8,128)S(1)}, f32[512,256]{1,0:T(8,128)S(1)}, u32[]{:S(2)}, u32[]{:S(2)}) collective-permute-start(f32[512,256]{1,0:T(8,128)S(1)} %get-tuple-element.32), channel_id=1, source_target_pairs={{0,1},{1,0},{2,3},{3,2},{4,5},{5,4},{6,7},{7,6},{8,9},{9,8},{10,11... | collective-permute-start | bytes 1572872 | tf_op jit(solution)/shard_map/ppermute | solution.py:406
  15.5 14.8 %collective-permute-start.5 = (f32[512,256]{1,0:T(8,128)S(1)}, f32[512,256]{1,0:T(8,128)S(1)}, u32[]{:S(2)}, u32[]{:S(2)}) collective-permute-start(f32[512,256]{1,0:T(8,128)S(1)} %add.42), channel_id=1, source_target_pairs={{0,2},{1,3},{2,4},{3,5},{4,6},{5,7},{6,0},{7,1},{8,10},{9,11},{10,... | collective-permute-start | bytes 1572872 | tf_op jit(solution)/shard_map/ppermute | solution.py:406
  17.0 13.4 %collective-permute-start.7 = (f32[512,256]{1,0:T(8,128)S(1)}, f32[512,256]{1,0:T(8,128)S(1)}, u32[]{:S(2)}, u32[]{:S(2)}) collective-permute-start(f32[512,256]{1,0:T(8,128)S(1)} %add.43), channel_id=1, source_target_pairs={{0,6},{1,7},{2,0},{3,1},{4,2},{5,3},{6,4},{7,5},{8,14},{9,15},{10,... | collective-permute-start | bytes 1572872 | tf_op jit(solution)/shard_map/ppermute | solution.py:406
  20.2 13.2 %collective-permute-start = (f32[512,256]{1,0:T(8,128)S(1)}, f32[512,256]{1,0:T(8,128)S(1)}, u32[]{:S(2)}, u32[]{:S(2)}) collective-permute-start(f32[512,256]{1,0:T(8,128)S(1)} %get-tuple-element.27), channel_id=1, source_target_pairs={{0,1},{1,0},{2,3},{3,2},{4,5},{5,4},{6,7},{7,6},{8,9},{9,8},{10,11... | collective-permute-start | bytes 1572872 | tf_op jit(solution)/shard_map/ppermute | solution.py:406
  22.7 12.0 %collective-permute-start.1 = (f32[512,256]{1,0:T(8,128)S(1)}, f32[512,256]{1,0:T(8,128)S(1)}, u32[]{:S(2)}, u32[]{:S(2)}) collective-permute-start(f32[512,256]{1,0:T(8,128)S(1)} %get-tuple-element.28), channel_id=1, source_target_pairs={{0,1},{1,0},{2,3},{3,2},{4,5},{5,4},{6,7},{7,6},{8,9},{9,8},{10,11... | collective-permute-start | bytes 1572872 | tf_op jit(solution)/shard_map/ppermute | solution.py:406
  22.9 18.7 %collective-permute-start.10 = (f32[512,256]{1,0:T(8,128)S(1)}, f32[512,256]{1,0:T(8,128)S(1)}, u32[]{:S(2)}, u32[]{:S(2)}) collective-permute-start(f32[512,256]{1,0:T(8,128)S(1)} %add.44), channel_id=1, source_target_pairs={{0,6},{1,7},{2,0},{3,1},{4,2},{5,3},{6,4},{7,5},{8,14},{9,15},{10,... | collective-permute-start | bytes 1572872 | tf_op jit(solution)/shard_map/ppermute | solution.py:406
  30.4 13.7 %collective-permute-start.12 = (f32[512,256]{1,0:T(8,128)S(1)}, f32[512,256]{1,0:T(8,128)S(1)}, u32[]{:S(2)}, u32[]{:S(2)}) collective-permute-start(f32[512,256]{1,0:T(8,128)S(1)} %add.45), channel_id=1, source_target_pairs={{0,2},{1,3},{2,4},{3,5},{4,6},{5,7},{6,0},{7,1},{8,10},{9,11},{10,... | collective-permute-start | bytes 1572872 | tf_op jit(solution)/shard_map/ppermute | solution.py:406
  31.9 23.3 %collective-permute-start.8 = (f32[512,256]{1,0:T(8,128)S(1)}, f32[512,256]{1,0:T(8,128)S(1)}, u32[]{:S(2)}, u32[]{:S(2)}) collective-permute-start(f32[512,256]{1,0:T(8,128)S(1)} %get-tuple-element.38), channel_id=1, source_target_pairs={{0,2},{1,3},{2,4},{3,5},{4,6},{5,7},{6,0},{7,1},{8,10},{9,11},{10,... | collective-permute-start | bytes 1572872 | tf_op jit(solution)/shard_map/ppermute | solution.py:406
  33.5 21.8 %collective-permute-start.13 = (f32[512,256]{1,0:T(8,128)S(1)}, f32[512,256]{1,0:T(8,128)S(1)}, u32[]{:S(2)}, u32[]{:S(2)}) collective-permute-start(f32[512,256]{1,0:T(8,128)S(1)} %get-tuple-element.44), channel_id=1, source_target_pairs={{0,6},{1,7},{2,0},{3,1},{4,2},{5,3},{6,4},{7,5},{8,14},{9,15},{10,... | collective-permute-start | bytes 1572872 | tf_op jit(solution)/shard_map/ppermute | solution.py:406
  58.8 6.1 %collective-permute-start.17 = (f32[136,128]{1,0:T(8,128)S(1)}, f32[136,128]{1,0:T(8,128)S(1)}, u32[]{:S(2)}, u32[]{:S(2)}) collective-permute-start(f32[136,128]{1,0:T(8,128)S(1)} %add.46), channel_id=1, source_target_pairs={{0,64},{1,17},{2,66},{3,19},{4,68},{5,21},{6,70},{7,23},{8,72},{9,... | collective-permute-start | bytes 208904 | tf_op jit(solution)/shard_map/ppermute | solution.py:440
  62.2 4.4 %collective-permute-start.16 = (f32[136,128]{1,0:T(8,128)S(1)}, f32[136,128]{1,0:T(8,128)S(1)}, u32[]{:S(2)}, u32[]{:S(2)}) collective-permute-start(f32[136,128]{1,0:T(8,128)S(1)} %add.46), channel_id=1, source_target_pairs={{0,32},{1,9},{2,34},{3,11},{4,36},{5,13},{6,38},{7,15},{8,40},{9,1... | collective-permute-start | bytes 208904 | tf_op jit(solution)/shard_map/ppermute | solution.py:440
  62.3 4.2 %collective-permute-start.15 = (f32[136,128]{1,0:T(8,128)S(1)}, f32[136,128]{1,0:T(8,128)S(1)}, u32[]{:S(2)}, u32[]{:S(2)}) collective-permute-start(f32[136,128]{1,0:T(8,128)S(1)} %add.46), channel_id=1, source_target_pairs={{0,96},{1,25},{2,98},{3,27},{4,100},{5,29},{6,102},{7,31},{8,104},... | collective-permute-start | bytes 208904 | tf_op jit(solution)/shard_map/ppermute | solution.py:440
  66.6 4.8 %collective-permute-start.20 = (f32[136,128]{1,0:T(8,128)S(1)}, f32[136,128]{1,0:T(8,128)S(1)}, u32[]{:S(2)}, u32[]{:S(2)}) collective-permute-start(f32[136,128]{1,0:T(8,128)S(1)} %add_add_fusion.2), channel_id=1, source_target_pairs={{0,16},{1,5},{2,18},{3,7},{4,20},{5,1},{6,22},{7,3},{8,24},{9,13},... | collective-permute-start | bytes 208904 | tf_op jit(solution)/shard_map/ppermute | solution.py:440
  67.3 4.7 %collective-permute-start.19 = (f32[136,128]{1,0:T(8,128)S(1)}, f32[136,128]{1,0:T(8,128)S(1)}, u32[]{:S(2)}, u32[]{:S(2)}) collective-permute-start(f32[136,128]{1,0:T(8,128)S(1)} %add_add_fusion.2), channel_id=1, source_target_pairs={{0,8},{1,3},{2,10},{3,5},{4,12},{5,7},{6,14},{7,1},{8,16},{9,11},{... | collective-permute-start | bytes 208904 | tf_op jit(solution)/shard_map/ppermute | solution.py:440
  67.3 4.7 %collective-permute-start.18 = (f32[136,128]{1,0:T(8,128)S(1)}, f32[136,128]{1,0:T(8,128)S(1)}, u32[]{:S(2)}, u32[]{:S(2)}) collective-permute-start(f32[136,128]{1,0:T(8,128)S(1)} %add_add_fusion.2), channel_id=1, source_target_pairs={{0,24},{1,7},{2,26},{3,1},{4,28},{5,3},{6,30},{7,5},{8,0},{9,15},{... | collective-permute-start | bytes 208904 | tf_op jit(solution)/shard_map/ppermute | solution.py:440
  72.1 6.1 %collective-permute-start.23 = (f32[136,128]{1,0:T(8,128)S(1)}, f32[136,128]{1,0:T(8,128)S(1)}, u32[]{:S(2)}, u32[]{:S(2)}) collective-permute-start(f32[136,128]{1,0:T(8,128)S(1)} %add_add_fusion.1), channel_id=1, source_target_pairs={{0,4},{1,65},{2,6},{3,67},{4,0},{5,69},{6,2},{7,71},{8,12},{9,73},... | collective-permute-start | bytes 208904 | tf_op jit(solution)/shard_map/ppermute | solution.py:440
  75.5 4.4 %collective-permute-start.22 = (f32[136,128]{1,0:T(8,128)S(1)}, f32[136,128]{1,0:T(8,128)S(1)}, u32[]{:S(2)}, u32[]{:S(2)}) collective-permute-start(f32[136,128]{1,0:T(8,128)S(1)} %add_add_fusion.1), channel_id=1, source_target_pairs={{0,2},{1,33},{2,4},{3,35},{4,6},{5,37},{6,0},{7,39},{8,10},{9,41},... | collective-permute-start | bytes 208904 | tf_op jit(solution)/shard_map/ppermute | solution.py:440
  76.2 3.7 %collective-permute-start.21 = (f32[136,128]{1,0:T(8,128)S(1)}, f32[136,128]{1,0:T(8,128)S(1)}, u32[]{:S(2)}, u32[]{:S(2)}) collective-permute-start(f32[136,128]{1,0:T(8,128)S(1)} %add_add_fusion.1), channel_id=1, source_target_pairs={{0,6},{1,97},{2,0},{3,99},{4,2},{5,101},{6,4},{7,103},{8,14},{9,10... | collective-permute-start | bytes 208904 | tf_op jit(solution)/shard_map/ppermute | solution.py:440
  79.9 5.3 %collective-permute-start.24 = (f32[136,128]{1,0:T(8,128)S(1)}, f32[136,128]{1,0:T(8,128)S(1)}, u32[]{:S(2)}, u32[]{:S(2)}) collective-permute-start(f32[136,128]{1,0:T(8,128)S(1)} %add_add_fusion.mine), channel_id=1, source_target_pairs={{0,1},{1,0},{2,3},{3,2},{4,5},{5,4},{6,7},{7,6},{8,9},{9,8},{10,11... | collective-permute-start | bytes 208904 | tf_op jit(solution)/shard_map/ppermute | solution.py:406
  (1 other events, 2.9 us)
